TPU v7x, 32 devices: a whole 2x2x4 slice. The times are simulated.
32 devices in a mesh: replica: 8 (over y, x, core), shard: 4 (over z).
Axes of the slice: x: 2, y: 2, z: 4, core: 2. Of those that a mesh axis runs over, the one named last changes fastest.
Arguments:
- tokens: bfloat16 [64, 197, 768], P(('replica', 'shard')), may hold values from -6 to 6
- expert_ids: int32 [64, 197, 2], P(('replica', 'shard')), may hold values from 0 to 3, all different within a row; in each aligned block of 394 rows (0 to 393, 394 to 787, ..., all dimensions but the last counted through in order) at most 264 rows name the same one
- qkv_weight: bfloat16 [3, 768, 2304], P(None, 'shard'), may hold values from -0.21875 to 0.21875
- out_weight: bfloat16 [3, 768, 768], P(None, 'shard'), may hold values from -0.875 to 0.875
- router_weight: bfloat16 [3, 768, 4], P(None, 'shard'), may hold values from -0.21875 to 0.21875
- norm_gain: float32 [3, 2, 768], replicated, may hold values from 0.5 to 1.5
- norm_shift: float32 [3, 2, 768], replicated, may hold values from -2 to 2
- expert_in: bfloat16 [3, 4, 768, 3072], P(None, 'shard'), may hold values from -0.21875 to 0.21875
- expert_out: bfloat16 [3, 4, 3072, 768], P(None, 'shard'), may hold values from -0.625 to 0.625
- cotangent: bfloat16 [64, 197, 768], P(('replica', 'shard')), may hold values from -6 to 6
Outputs:
- activations: bfloat16 [64, 197, 768], P(('replica', 'shard'))
- input_grad: float32 [64, 197, 768], P(('replica', 'shard'))
- qkv_grad: float32 [3, 768, 2304], P(None, 'shard')
- out_grad: float32 [3, 768, 768], P(None, 'shard')
- router_grad: float32 [3, 768, 4], P(None, 'shard')
- gain_grad: float32 [3, 2, 768], P(None, None, 'shard')
- shift_grad: float32 [3, 2, 768], P(None, None, 'shard')
- expert_in_grad: float32 [3, 4, 768, 3072], P(None, 'shard', None, 'replica')
- expert_out_grad: float32 [3, 4, 3072, 768], P(None, 'shard', 'replica')
Inputs may be any that keep to these rules, and one draw needn't show every extreme that they name: `expert_ids`: the two ids of a token differ. Among the 394 tokens of one device no expert is named more than 264 times, and in every draw some device names some expert exactly 264 times.
All inputs are finite; a program needn't handle non-finite values.
Results may differ from a plain program's by a relative error of at most 0.025.
Values may be sent and summed in bfloat16 or wider, within the bound.
No kernel may reach another device: no remote copies, remote signals or barrier semaphores. Data moves between devices by JAX's collectives and lax.ppermute only.
A program may use at most 384 MiB of HBM per device.

v0:
```python
import jax
import jax.numpy as jnp
from jax import lax
from jax.sharding import PartitionSpec as P

HEAD = 64
EXP_DEV = 1
LAYERS = 3


eps_norm = 1e-06
inv_root_two = 0.7071067811865476
inv_root_two_pi = 0.3989422804014327


def norm_parts(values_in):
    average = jnp.mean(values_in, axis=-1, keepdims=True)
    centred = values_in - average
    variance = jnp.mean(centred * centred, axis=-1, keepdims=True)
    inverse = lax.rsqrt(variance + eps_norm)
    return (centred * inverse, inverse)


def norm_back(grad_out, normed, inverse, gain_row):
    scaled = grad_out * gain_row
    inner = jnp.mean(scaled, axis=-1, keepdims=True)
    along = jnp.mean(scaled * normed, axis=-1, keepdims=True)
    grad_in = inverse * (scaled - inner - normed * along)
    return (grad_in, jnp.sum(grad_out * normed, axis=0), jnp.sum(grad_out, axis=0))


def gelu_slope(pre_act):
    return (
        0.5 * (1.0 + lax.erf(pre_act * inv_root_two))
        + pre_act * jnp.exp(-0.5 * pre_act * pre_act) * inv_root_two_pi
    )


def split_heads(qkv_rows, images, length, head_count):
    features = qkv_rows.shape[1] // 3
    head_size = features // head_count
    queries = qkv_rows[:, :features].reshape(images, length, head_count, head_size)
    key_rows = qkv_rows[:, features : 2 * features].reshape(images, length, head_count, head_size)
    value_rows = qkv_rows[:, 2 * features :].reshape(images, length, head_count, head_size)
    return (queries, key_rows, value_rows)


def attend(queries, key_rows):
    scores = jnp.einsum(
        "bqhd,bkhd->bhqk", queries, key_rows, preferred_element_type=jnp.float32
    ) * queries.shape[-1] ** (-0.5)
    highest = jnp.max(scores, axis=-1, keepdims=True)
    raised = jnp.exp(scores - highest)
    row_total = jnp.sum(raised, axis=-1, keepdims=True)
    return (raised / row_total, highest + jnp.log(row_total))


def forward_layer(
    residual, dense_set, gains, shifts, first_weight, second_weight, ids_pair, positions, shape_info
):
    images, length, head_count, experts, capacity = shape_info
    qkv_w, out_w, router_w = dense_set
    token_count, features = residual.shape
    normed_one, inverse_one = norm_parts(residual)
    hidden_one = (normed_one * gains[0] + shifts[0]).astype(jnp.bfloat16)
    qkv_rows = jnp.dot(hidden_one, qkv_w, preferred_element_type=jnp.float32).astype(jnp.bfloat16)
    queries, key_rows, value_rows = split_heads(qkv_rows, images, length, head_count)
    attn_weights, log_total = attend(queries, key_rows)
    context = (
        jnp.einsum(
            "bhqk,bkhd->bqhd",
            attn_weights.astype(jnp.bfloat16),
            value_rows,
            preferred_element_type=jnp.float32,
        )
        .astype(jnp.bfloat16)
        .reshape(token_count, features)
    )
    middle = residual + jnp.dot(context, out_w, preferred_element_type=jnp.float32)
    normed_two, inverse_two = norm_parts(middle)
    hidden_two = (normed_two * gains[1] + shifts[1]).astype(jnp.bfloat16)
    router = jax.nn.softmax(
        jnp.dot(hidden_two, router_w, preferred_element_type=jnp.float32), axis=-1
    )
    gate_values = jnp.take_along_axis(router, ids_pair, axis=1)
    doubled = jnp.repeat(hidden_two, 2, axis=0)
    buffer = jnp.zeros((experts * capacity, features), jnp.bfloat16).at[positions].set(doubled)
    arrived = lax.all_to_all(
        buffer.reshape(experts, capacity, features),
        "shard",
        split_axis=0,
        concat_axis=1,
        tiled=True,
    )
    pre_act = jnp.einsum("emd,edf->emf", arrived, first_weight, preferred_element_type=jnp.float32)
    activated = jax.nn.gelu(pre_act, approximate=False).astype(jnp.bfloat16)
    produced = jnp.einsum(
        "emf,efd->emd", activated, second_weight, preferred_element_type=jnp.float32
    ).astype(jnp.bfloat16)
    returned = lax.all_to_all(produced, "shard", split_axis=1, concat_axis=0, tiled=True)
    picked = (
        returned.reshape(experts * capacity, features)[positions]
        .astype(jnp.float32)
        .reshape(token_count, 2, features)
    )
    residual_next = middle + jnp.sum(gate_values[:, :, None] * picked, axis=1)
    record = (
        normed_one,
        inverse_one,
        hidden_one,
        qkv_rows,
        log_total,
        context,
        normed_two,
        inverse_two,
        hidden_two,
        router,
        gate_values,
        arrived,
        pre_act,
        activated,
        picked,
    )
    return (record, residual_next)


def backward_layer(
    gradient, record, dense_set, gains, first_weight, second_weight, positions, choose, shape_info
):
    images, length, head_count, experts, capacity = shape_info
    (
        normed_one,
        inverse_one,
        hidden_one,
        qkv_rows,
        log_total,
        context,
        normed_two,
        inverse_two,
        hidden_two,
        router,
        gate_values,
        arrived,
        pre_act,
        activated,
        picked,
    ) = record
    qkv_w, out_w, router_w = dense_set
    token_count, features = gradient.shape
    grad_gates = jnp.sum(gradient[:, None, :] * picked, axis=2)
    spread = (gate_values[:, :, None] * gradient[:, None, :]).reshape(2 * token_count, features)
    grad_slots = (
        jnp.zeros((experts * capacity, features), jnp.float32)
        .at[positions]
        .set(spread)
        .astype(jnp.bfloat16)
    )
    grad_arrived = lax.all_to_all(
        grad_slots.reshape(experts, capacity, features),
        "shard",
        split_axis=0,
        concat_axis=1,
        tiled=True,
    )
    grad_act = jnp.einsum(
        "emd,efd->emf", grad_arrived, second_weight, preferred_element_type=jnp.float32
    )
    grad_pre = (grad_act * gelu_slope(pre_act)).astype(jnp.bfloat16)
    grad_rows = jnp.einsum(
        "emf,edf->emd", grad_pre, first_weight, preferred_element_type=jnp.float32
    ).astype(jnp.bfloat16)
    grad_back = lax.all_to_all(grad_rows, "shard", split_axis=1, concat_axis=0, tiled=True)
    grad_two = jnp.sum(
        grad_back.reshape(experts * capacity, features)[positions]
        .astype(jnp.float32)
        .reshape(token_count, 2, features),
        axis=1,
    )
    grad_router = jnp.sum(choose * grad_gates[:, :, None], axis=1)
    grad_logits = (
        router * (grad_router - jnp.sum(router * grad_router, axis=-1, keepdims=True))
    ).astype(jnp.bfloat16)
    grad_router_w = jnp.einsum(
        "td,te->de", hidden_two, grad_logits, preferred_element_type=jnp.float32
    )
    grad_two = grad_two + jnp.einsum(
        "te,de->td", grad_logits, router_w, preferred_element_type=jnp.float32
    )
    grad_norm_two, gain_two, shift_two = norm_back(grad_two, normed_two, inverse_two, gains[1])
    grad_middle = gradient + grad_norm_two
    grad_attn = grad_middle.astype(jnp.bfloat16)
    grad_out_w = jnp.einsum("te,td->ed", context, grad_attn, preferred_element_type=jnp.float32)
    queries, key_rows, value_rows = split_heads(qkv_rows, images, length, head_count)
    grad_context = (
        jnp.einsum("td,ed->te", grad_attn, out_w, preferred_element_type=jnp.float32)
        .astype(jnp.bfloat16)
        .reshape(queries.shape)
    )
    score_scale = queries.shape[-1] ** (-0.5)
    scores = (
        jnp.einsum("bqhd,bkhd->bhqk", queries, key_rows, preferred_element_type=jnp.float32)
        * score_scale
    )
    attn_weights = jnp.exp(scores - log_total)
    grad_weights = jnp.einsum(
        "bqhd,bkhd->bhqk", grad_context, value_rows, preferred_element_type=jnp.float32
    )
    grad_values = jnp.einsum(
        "bhqk,bqhd->bkhd",
        attn_weights.astype(jnp.bfloat16),
        grad_context,
        preferred_element_type=jnp.float32,
    )
    grad_scores = (
        attn_weights * (grad_weights - jnp.sum(attn_weights * grad_weights, axis=-1, keepdims=True))
    ).astype(jnp.bfloat16)
    grad_queries = (
        jnp.einsum("bhqk,bkhd->bqhd", grad_scores, key_rows, preferred_element_type=jnp.float32)
        * score_scale
    )
    grad_keys = (
        jnp.einsum("bhqk,bqhd->bkhd", grad_scores, queries, preferred_element_type=jnp.float32)
        * score_scale
    )
    grad_qkv = jnp.concatenate(
        [
            grad_queries.reshape(token_count, features),
            grad_keys.reshape(token_count, features),
            grad_values.reshape(token_count, features),
        ],
        axis=1,
    ).astype(jnp.bfloat16)
    grad_qkv_w = jnp.einsum("td,te->de", hidden_one, grad_qkv, preferred_element_type=jnp.float32)
    grad_one = jnp.einsum("te,de->td", grad_qkv, qkv_w, preferred_element_type=jnp.float32)
    grad_norm_one, gain_one, shift_one = norm_back(grad_one, normed_one, inverse_one, gains[0])
    dense_terms = (
        grad_qkv_w,
        grad_out_w,
        grad_router_w,
        jnp.stack([gain_one, gain_two]),
        jnp.stack([shift_one, shift_two]),
    )
    expert_terms = (arrived, grad_pre, activated, grad_arrived)
    return (grad_middle + grad_norm_one, dense_terms, expert_terms)


def shards(
    tokens,
    expert_ids,
    qkv_weight,
    out_weight,
    router_weight,
    norm_gain,
    norm_shift,
    expert_in,
    expert_out,
    cotangent,
):
    images, length, features = tokens.shape
    token_count = images * length
    head_count = features // HEAD
    experts = EXP_DEV * lax.axis_size("shard")
    capacity = (8 * token_count + 24 * experts - 1) // (24 * experts) * 8
    ids_pair = expert_ids.reshape(token_count, 2)
    ids_flat = ids_pair.reshape(-1)
    labels = jnp.arange(experts, dtype=jnp.int32)
    member = (ids_flat[:, None] == labels[None, :]).astype(jnp.int32)
    earlier = jnp.cumsum(member, axis=0) - member
    positions = ids_flat * capacity + jnp.sum(earlier * member, axis=1)
    choose = (ids_pair[:, :, None] == labels[None, None, :]).astype(jnp.float32)
    shape_info = (images, length, head_count, experts, capacity)
    residual = tokens.reshape(token_count, features).astype(jnp.float32)
    records = []
    for layer_index in range(LAYERS):
        dense_set = (
            lax.all_gather(qkv_weight[layer_index], "shard", axis=0, tiled=True),
            lax.all_gather(out_weight[layer_index], "shard", axis=0, tiled=True),
            lax.all_gather(router_weight[layer_index], "shard", axis=0, tiled=True),
        )
        record, residual = forward_layer(
            residual,
            dense_set,
            norm_gain[layer_index],
            norm_shift[layer_index],
            expert_in[layer_index],
            expert_out[layer_index],
            ids_pair,
            positions,
            shape_info,
        )
        records.append((record, None))
    activations = residual.astype(jnp.bfloat16).reshape(images, length, features)
    gradient = cotangent.reshape(token_count, features).astype(jnp.float32)
    dense_out = [None] * LAYERS
    expert_sums = [None] * LAYERS
    for layer_index in range(LAYERS - 1, -1, -1):
        record, kept_set = records[layer_index]
        dense_set = (
            lax.all_gather(qkv_weight[layer_index], "shard", axis=0, tiled=True),
            lax.all_gather(out_weight[layer_index], "shard", axis=0, tiled=True),
            lax.all_gather(router_weight[layer_index], "shard", axis=0, tiled=True),
        )
        gradient, dense_terms, expert_terms = backward_layer(
            gradient,
            record,
            dense_set,
            norm_gain[layer_index],
            expert_in[layer_index],
            expert_out[layer_index],
            positions,
            choose,
            shape_info,
        )
        summed = (
            lax.psum_scatter(
                dense_terms[0].astype(jnp.bfloat16), "shard", scatter_dimension=0, tiled=True
            ).astype(jnp.float32),
            lax.psum_scatter(
                dense_terms[1].astype(jnp.bfloat16), "shard", scatter_dimension=0, tiled=True
            ).astype(jnp.float32),
            lax.psum_scatter(
                dense_terms[2].astype(jnp.bfloat16), "shard", scatter_dimension=0, tiled=True
            ).astype(jnp.float32),
            lax.psum_scatter(
                dense_terms[3].astype(jnp.bfloat16), "shard", scatter_dimension=1, tiled=True
            ).astype(jnp.float32),
            lax.psum_scatter(
                dense_terms[4].astype(jnp.bfloat16), "shard", scatter_dimension=1, tiled=True
            ).astype(jnp.float32),
        )
        dense_out[layer_index] = (
            lax.psum(summed[0].astype(jnp.bfloat16), "replica").astype(jnp.float32),
            lax.psum(summed[1].astype(jnp.bfloat16), "replica").astype(jnp.float32),
            lax.psum(summed[2].astype(jnp.bfloat16), "replica").astype(jnp.float32),
            lax.psum(summed[3].astype(jnp.bfloat16), "replica").astype(jnp.float32),
            lax.psum(summed[4].astype(jnp.bfloat16), "replica").astype(jnp.float32),
        )
        arrived, grad_pre, activated, grad_arrived = expert_terms
        local_first = jnp.einsum(
            "emd,emf->edf", arrived, grad_pre, preferred_element_type=jnp.float32
        )
        local_second = jnp.einsum(
            "emf,emd->efd", activated, grad_arrived, preferred_element_type=jnp.float32
        )
        expert_sums[layer_index] = (
            lax.psum_scatter(
                local_first.astype(jnp.bfloat16), "replica", scatter_dimension=2, tiled=True
            ).astype(jnp.float32),
            lax.psum_scatter(
                local_second.astype(jnp.bfloat16), "replica", scatter_dimension=1, tiled=True
            ).astype(jnp.float32),
        )
    input_grad = gradient.reshape(images, length, features)
    qkv_grad = jnp.stack([dense_out[index][0] for index in range(LAYERS)])
    out_grad = jnp.stack([dense_out[index][1] for index in range(LAYERS)])
    router_grad = jnp.stack([dense_out[index][2] for index in range(LAYERS)])
    gain_grad = jnp.stack([dense_out[index][3] for index in range(LAYERS)])
    shift_grad = jnp.stack([dense_out[index][4] for index in range(LAYERS)])
    expert_in_grad = jnp.stack([expert_sums[index][0] for index in range(LAYERS)])
    expert_out_grad = jnp.stack([expert_sums[index][1] for index in range(LAYERS)])
    return (
        activations,
        input_grad,
        qkv_grad,
        out_grad,
        router_grad,
        gain_grad,
        shift_grad,
        expert_in_grad,
        expert_out_grad,
    )


def solution(mesh):
    in_specs = (
        P(("replica", "shard"), None, None),
        P(("replica", "shard"), None, None),
        P(None, "shard", None),
        P(None, "shard", None),
        P(None, "shard", None),
        P(),
        P(),
        P(None, "shard", None, None),
        P(None, "shard", None, None),
        P(("replica", "shard"), None, None),
    )
    out_specs = (
        P(("replica", "shard"), None, None),
        P(("replica", "shard"), None, None),
        P(None, "shard", None),
        P(None, "shard", None),
        P(None, "shard", None),
        P(None, None, "shard"),
        P(None, None, "shard"),
        P(None, "shard", None, "replica"),
        P(None, "shard", "replica", None),
    )
    return jax.shard_map(shards, mesh=mesh, in_specs=in_specs, out_specs=out_specs, check_vma=False)
```

profile of v0, /device:TPU:0, one launch (start us, length us, event | category | flops | bytes accessed | tf_op | source)
XLA Modules:
  0.0 2005.6 jit_solution(8978492207210367422)
XLA Ops:
  17.8 65.6 %all-gather.16.cloned.1.call-done = bf16[1,768,2304]{2,1,0:T(8,128)(2,1)} async-done(((bf16[1,192,2304]{2,1,0:T(8,128)(2,1)}), bf16[1,768,2304]{2,1,0:T(8,128)(2,1)}) %all-gather.16.cloned.1.call-update) | async-done | bytes 3538960 | tf_op jit(solution)/shard_map/all_gather | solution.py:276
  106.9 7.5 all-gather.18.cloned.1.call-done
  119.8 6.9 scatter_custom_fusion
  131.1 69.3 %all-to-all-done = bf16[4,264,768]{2,1,0:T(8,128)(2,1)S(1)} async-done(((bf16[4,264,768]{2,1,0:T(8,128)(2,1)}), bf16[4,264,768]{2,1,0:T(8,128)(2,1)S(1)}, u32[]{:S(2)}, u32[]{:S(2)}) %all-to-all-start) | async-done | bytes 1622048 | tf_op jit(solution)/shard_map/all_to_all | solution.py:88
  200.3 36.3 %fusion.2 = (bf16[1056,3072]{1,0:T(8,128)(2,1)S(1)}, f32[1056,3072]{1,0:T(8,128)}) fusion(bf16[1056,768]{1,0:T(8,128)(2,1)S(1)} %bitcast.444, bf16[3,1,768,3072]{3,2,1,0:T(8,128)(2,1)} %param.19), kind=kOutput, calls=%fused_computation.26 | convolution fusion | flops 5193695232 | bytes 25804800 | tf_op jit(solution)/shard_map/emd,edf->emf/dot_general | solution.py:95
  236.7 9.9 fusion.129
  246.6 8.6 copy.717
  255.7 10.6 reduce.42
  275.6 61.8 %all-gather.2 = bf16[1,768,4]{2,0,1:T(2,128)(2,1)S(1)} all-gather(bf16[1,192,4]{2,0,1:T(2,128)(2,1)S(1)} %copy.680), channel_id=4, replica_groups=mesh['replica'=8,'shard'=4] {'shard'}, dimensions={1}, use_global_device_ids=true | all-gather | bytes 7680 | tf_op jit(solution)/shard_map/all_gather | solution.py:278
  338.8 10.6 gather_fusion.6
  391.7 6.9 scatter_custom_fusion.1
  403.4 67.5 %all-to-all-done.2 = bf16[4,264,768]{2,1,0:T(8,128)(2,1)S(1)} async-done(((bf16[4,264,768]{2,1,0:T(8,128)(2,1)}), bf16[4,264,768]{2,1,0:T(8,128)(2,1)S(1)}, u32[]{:S(2)}, u32[]{:S(2)}) %all-to-all-start.2) | async-done | bytes 1622048 | tf_op jit(solution)/shard_map/all_to_all | solution.py:88
  470.9 36.3 %fusion.5 = (bf16[1056,3072]{1,0:T(8,128)(2,1)S(1)}, f32[1056,3072]{1,0:T(8,128)}) fusion(bf16[1056,768]{1,0:T(8,128)(2,1)S(1)} %bitcast.446, bf16[3,1,768,3072]{3,2,1,0:T(8,128)(2,1)} %param.19), kind=kOutput, calls=%fused_computation.29 | convolution fusion | flops 5193695232 | bytes 25804800 | tf_op jit(solution)/shard_map/emd,edf->emf/dot_general | solution.py:95
  507.2 9.9 fusion.123
  517.1 8.6 copy.716
  525.7 10.6 reduce.43
  544.8 59.3 %all-gather.5 = bf16[1,768,4]{2,0,1:T(2,128)(2,1)S(1)} all-gather(bf16[1,192,4]{2,0,1:T(2,128)(2,1)S(1)} %copy.681), channel_id=7, replica_groups=mesh['replica'=8,'shard'=4] {'shard'}, dimensions={1}, use_global_device_ids=true | all-gather | bytes 7680 | tf_op jit(solution)/shard_map/all_gather | solution.py:278
  605.6 10.6 gather_fusion.7
  660.2 7.0 scatter_custom_fusion.2
  671.9 39.4 %all-gather.8 = bf16[1,768,4]{2,0,1:T(2,128)(2,1)S(1)} all-gather(bf16[1,192,4]{2,0,1:T(2,128)(2,1)S(1)} %copy.682), channel_id=10, replica_groups=mesh['replica'=8,'shard'=4] {'shard'}, dimensions={1}, use_global_device_ids=true | all-gather | bytes 7680 | tf_op jit(solution)/shard_map/all_gather | solution.py:278
  719.2 10.6 gather_fusion.8
  731.1 10.1 scatter_custom_fusion.3
  746.7 36.7 %fusion.8 = (bf16[1056,3072]{1,0:T(8,128)(2,1)}, f32[1056,3072]{1,0:T(8,128)}) fusion(bf16[1056,768]{1,0:T(8,128)(2,1)} %bitcast.27, bf16[3,1,768,3072]{3,2,1,0:T(8,128)(2,1)} %param.19), kind=kOutput, calls=%fused_computation.32 | convolution fusion | flops 5193695232 | bytes 25804800 | tf_op jit(solution)/shard_map/emd,edf->emf/dot_general | solution.py:95
  783.5 11.3 fusion.42
  794.8 9.9 fusion.120
  804.7 8.6 copy.714
  813.3 10.6 reduce.44
  832.7 8.7 fusion.117
  841.4 8.6 copy.715
  850.0 10.6 reduce.45
  887.7 13.3 all-to-all-done.5
  915.7 8.1 multiply_reduce_fusion.8
  960.0 10.1 scatter_custom_fusion.4
  983.1 30.7 %all-to-all-done.8 = bf16[4,264,768]{2,1,0:T(8,128)(2,1)} async-done(((bf16[4,264,768]{2,1,0:T(8,128)(2,1)}), bf16[4,264,768]{2,1,0:T(8,128)(2,1)}, u32[]{:S(2)}, u32[]{:S(2)}) %all-to-all-start.8) | async-done | bytes 1622048 | tf_op jit(solution)/shard_map/all_to_all | solution.py:158
  1013.9 11.4 fusion.43
  1025.3 9.9 fusion.126
  1035.2 8.6 copy.713
  1043.8 10.6 reduce.46
  1061.7 10.4 fusion.68
  1072.1 20.5 %copy.645 = bf16[1,768,3072]{1,0,2:T(2,128)(2,1)} copy(bf16[1,768,3072]{2,1,0:T(8,128)(2,1)} %fusion.68) | data formatting | bytes 9437184
  1176.7 11.2 scatter_custom_fusion.5
  1204.7 31.5 %all-to-all-done.10 = bf16[4,264,768]{2,1,0:T(8,128)(2,1)} async-done(((bf16[4,264,768]{2,1,0:T(8,128)(2,1)}), bf16[4,264,768]{2,1,0:T(8,128)(2,1)}, u32[]{:S(2)}, u32[]{:S(2)}) %all-to-all-start.10) | async-done | bytes 1622048 | tf_op jit(solution)/shard_map/all_to_all | solution.py:158
  1236.2 11.6 fusion.44
  1247.8 9.9 fusion.132
  1257.8 12.5 copy.712
  1270.3 10.5 reduce.47
  1286.3 77.5 %all-to-all-done.11 = bf16[4,2,101376]{2,1,0:T(2,128)(2,1)S(1)} async-done(((bf16[4,2,101376]{2,1,0:T(2,128)(2,1)}), bf16[4,2,101376]{2,1,0:T(2,128)(2,1)S(1)}, u32[]{:S(2)}, u32[]{:S(2)}) %all-to-all-start.11) | async-done | bytes 1622048 | tf_op jit(solution)/shard_map/all_to_all | solution.py:172
  1424.2 10.8 fusion.67
  1435.0 20.4 %copy.643 = bf16[1,768,3072]{1,0,2:T(2,128)(2,1)} copy(bf16[1,768,3072]{2,1,0:T(8,128)(2,1)} %fusion.67) | data formatting | bytes 9437184
  1470.4 10.8 fusion.66
  1481.2 20.5 %copy.641 = bf16[1,768,3072]{1,0,2:T(2,128)(2,1)} copy(bf16[1,768,3072]{2,1,0:T(8,128)(2,1)} %fusion.66) | data formatting | bytes 9437184
  1509.7 11.0 fusion.71
  1520.9 10.5 fusion.70
  1531.5 10.5 fusion.69
  1554.2 34.9 %reduce-scatter.46.cloned.1.call-done = bf16[192,2304]{1,0:T(8,128)(2,1)} async-done(((bf16[768,2304]{1,0:T(8,128)(2,1)}), bf16[192,2304]{1,0:T(8,128)(2,1)}) %reduce-scatter.46.cloned.1.call-update) | async-done | bytes 884752 | tf_op jit(solution)/shard_map/reduce_scatter | solution.py:315
  1589.1 57.4 %reduce-scatter.84.cloned.1.call-done = bf16[384,768]{1,0:T(8,128)(2,1)} async-done(((bf16[3072,768]{1,0:T(8,128)(2,1)}), bf16[384,768]{1,0:T(8,128)(2,1)}) %reduce-scatter.84.cloned.1.call-update) | async-done | bytes 589840
  1659.5 8.9 reduce-scatter.76.cloned.1.call-done
  1669.3 19.3 reduce-scatter.70.cloned.1.call-done
  1689.4 22.6 %all-reduce.1 = (bf16[1,192,4]{1,2,0:T(4,128)(2,1)S(1)}, bf16[1,192,4]{1,2,0:T(4,128)(2,1)S(1)}, bf16[1,192,4]{1,2,0:T(4,128)(2,1)S(1)}, bf16[1,2,192]{2,1,0:T(2...) all-reduce(bf16[1,192,4]{1,2,0:T(4,128)(2,1)S(1)} %bitcast.473, ...), channel_id=1, replica_groups=mesh['replica'=8,'shard'=4] {'replica'}, use_global_device_ids=true, to_apply=%region_80.82 | all-reduce | flops 4608 | bytes 18432 | tf_op jit(solution)/shard_map/psum | solution.py:334
  1713.8 30.1 %reduce-scatter.82.cloned.1.call-done = bf16[384,768]{1,0:T(8,128)(2,1)} async-done(((bf16[3072,768]{1,0:T(8,128)(2,1)}), bf16[384,768]{1,0:T(8,128)(2,1)}) %reduce-scatter.82.cloned.1.call-update) | async-done | bytes 589840
  1747.2 53.9 %reduce-scatter.62.cloned.1.call-done = bf16[1,384,768]{2,1,0:T(8,128)(2,1)} async-done(((bf16[1,3072,768]{2,1,0:T(8,128)(2,1)}), bf16[1,384,768]{2,1,0:T(8,128)(2,1)}) %reduce-scatter.62.cloned.1.call-update) | async-done | bytes 589840 | tf_op jit(solution)/shard_map/reduce_scatter | solution.py:349
  1801.1 57.1 %reduce-scatter.60.cloned.1.call-done = bf16[1,384,768]{2,1,0:T(8,128)(2,1)} async-done(((bf16[1,3072,768]{2,1,0:T(8,128)(2,1)}), bf16[1,384,768]{2,1,0:T(8,128)(2,1)}) %reduce-scatter.60.cloned.1.call-update) | async-done | bytes 589840 | tf_op jit(solution)/shard_map/reduce_scatter | solution.py:349
  1858.2 57.1 %reduce-scatter.58.cloned.1.call-done = bf16[1,384,768]{2,1,0:T(8,128)(2,1)} async-done(((bf16[1,3072,768]{2,1,0:T(8,128)(2,1)}), bf16[1,384,768]{2,1,0:T(8,128)(2,1)}) %reduce-scatter.58.cloned.1.call-update) | async-done | bytes 589840 | tf_op jit(solution)/shard_map/reduce_scatter | solution.py:349
  1920.9 72.2 %all-reduce.5.cloned.1.call-done = (bf16[1,192,2304]{2,1,0:T(8,128)(2,1)}, bf16[1,192,2304]{2,1,0:T(8,128)(2,1)}, bf16[1,192,2304]{2,1,0:T(8,128)(2,1)}, bf16[1,...) async-done(((bf16[1,192,2304]{2,1,0:T(8,128)(2,1)}, bf16[1,192,2304]{2,1,0:T(8,128)(2,1)}, bf16[1,192,2304]{2,1,0:T(8,128)(2,1)}, ...) | async-done | bytes 3538960 | tf_op jit(solution)/shard_map/psum | solution.py:332
  (833 shorter events, 512.7 us)
Async XLA Ops:
  7.2 76.2 %all-gather.16.cloned.1.call-start = ((), (), s32[]{:S(2)}) async-start(), calls=%async_computation.42 | async-start | bytes 4423680 | tf_op jit(solution)/shard_map/all_gather | solution.py:276
  10.6 103.8 %all-gather.18.cloned.1.call-start = ((), (), s32[]{:S(2)}) async-start(), calls=%async_computation.43 | async-start | bytes 1474560 | tf_op jit(solution)/shard_map/all_gather | solution.py:277
  14.5 72.6 %copy-start.171 = (f32[768]{0:T(1024)}, f32[768]{0:T(1024)S(1)}, u32[]{:S(2)}) copy-start(f32[768]{0:T(1024)S(1)} %get-tuple-element.103) | copy-start | bytes 9220
  14.5 102.3 %copy-start.129 = (f32[768]{0:T(1024)}, f32[768]{0:T(1024)S(1)}, u32[]{:S(2)}) copy-start(f32[768]{0:T(1024)S(1)} %get-tuple-element.102) | copy-start | bytes 9220
  15.1 72.0 %copy-start.188 = (f32[768]{0:T(1024)}, f32[768]{0:T(1024)S(1)}, u32[]{:S(2)}) copy-start(f32[768]{0:T(1024)S(1)} %get-tuple-element.109) | copy-start | bytes 9220
  15.2 71.9 %copy-start.177 = (f32[394]{0:T(512)}, f32[394]{0:T(512)S(1)}, u32[]{:S(2)}) copy-start(f32[394]{0:T(512)S(1)} %div.123) | copy-start | bytes 4732
  15.4 71.7 %copy-start.179 = (f32[394]{0:T(512)}, f32[394]{0:T(512)S(1)}, u32[]{:S(2)}) copy-start(f32[394]{0:T(512)S(1)} %rsqrt.52) | copy-start | bytes 4732
  17.7 96.7 %copy-start.30 = (f32[394,768]{1,0:T(8,128)}, f32[394,768]{1,0:T(8,128)S(1)}, u32[]{:S(2)}) copy-start(f32[394,768]{1,0:T(8,128)S(1)} %reshape.962) | copy-start | bytes 3631108
  17.7 102.1 %copy-start.169 = (s32[788]{0:T(1024)}, s32[788]{0:T(1024)S(1)}, u32[]{:S(2)}) copy-start(s32[788]{0:T(1024)S(1)} %fusion.227) | copy-start | bytes 9460
  126.7 73.6 %all-to-all-start = ((bf16[4,264,768]{2,1,0:T(8,128)(2,1)}), bf16[4,264,768]{2,1,0:T(8,128)(2,1)S(1)}, u32[]{:S(2)}, u32[]{:S(2)}) async-start(bf16[4,264,768]{2,1,0:T(8,128)(2,1)} %bitcast.6), calls=%async_computation | async-start | bytes 3244032 | tf_op jit(solution)/shard_map/all_to_all | solution.py:88
  130.3 236.0 %all-gather.20.cloned.1.call-start = ((), (), s32[]{:S(2)}) async-start(), calls=%async_computation.44 | async-start | bytes 4423680 | tf_op jit(solution)/shard_map/all_gather | solution.py:276
  200.3 36.3 %copy-start.85 = (bf16[4,264,768]{2,1,0:T(8,128)(2,1)}, bf16[4,264,768]{2,1,0:T(8,128)(2,1)S(1)}, u32[]{:S(2)}) copy-start(bf16[4,264,768]{2,1,0:T(8,128)(2,1)S(1)} %all-to-all-done) | copy-start | bytes 4866052
  270.0 67.7 %copy-start.170 = (s32[788]{0:T(1024)S(1)}, s32[788]{0:T(1024)}, u32[]{:S(2)}) copy-start(s32[788]{0:T(1024)} %copy-done.169) | copy-start | bytes 9460
  270.0 67.8 %copy-start.40 = (bf16[394,768]{1,0:T(8,128)(2,1)S(1)}, bf16[394,768]{1,0:T(8,128)(2,1)}, u32[]{:S(2)}) copy-start(bf16[394,768]{1,0:T(8,128)(2,1)} %copy-done.39) | copy-start | bytes 1815556
  270.1 79.8 %all-to-all-start.1 = ((bf16[4,2,101376]{2,1,0:T(2,128)(2,1)}), bf16[4,2,101376]{2,1,0:T(2,128)(2,1)S(1)}, u32[]{:S(2)}, u32[]{:S(2)}) async-start(bf16[4,2,101376]{2,1,0:T(2,128)(2,1)} %reshape.1189), calls=%async_computation.1 | async-start | bytes 3244032 | tf_op jit(solution)/shard_map/all_to_all | solution.py:100
  273.8 112.3 %all-gather.22.cloned.1.call-start = ((), (), s32[]{:S(2)}) async-start(), calls=%async_computation.45 | async-start | bytes 1474560 | tf_op jit(solution)/shard_map/all_gather | solution.py:277
  274.5 75.2 %copy-start.111 = (s32[394,2]{0,1:T(2,128)}, s32[394,2]{0,1:T(2,128)S(1)}, u32[]{:S(2)}) copy-start(s32[394,2]{0,1:T(2,128)S(1)} %reshape.908) | copy-start | bytes 9460
  275.5 73.8 %copy-start = (s32[788]{0:T(1024)}, s32[788]{0:T(1024)S(1)}, u32[]{:S(2)}) copy-start(s32[788]{0:T(1024)S(1)} %reshape.1110) | copy-start | bytes 9460
  337.8 11.6 copy-start.135
  337.8 16.9 copy-start.114
  349.8 11.9 copy-start.79
  398.6 72.3 %all-to-all-start.2 = ((bf16[4,264,768]{2,1,0:T(8,128)(2,1)}), bf16[4,264,768]{2,1,0:T(8,128)(2,1)S(1)}, u32[]{:S(2)}, u32[]{:S(2)}) async-start(bf16[4,264,768]{2,1,0:T(8,128)(2,1)} %bitcast.16), calls=%async_computation.2 | async-start | bytes 3244032 | tf_op jit(solution)/shard_map/all_to_all | solution.py:88
  402.8 230.3 %all-gather.24.cloned.1.call-start = ((), (), s32[]{:S(2)}) async-start(), calls=%async_computation.46 | async-start | bytes 4423680 | tf_op jit(solution)/shard_map/all_gather | solution.py:276
  470.9 36.3 %copy-start.87 = (bf16[4,264,768]{2,1,0:T(8,128)(2,1)}, bf16[4,264,768]{2,1,0:T(8,128)(2,1)S(1)}, u32[]{:S(2)}) copy-start(bf16[4,264,768]{2,1,0:T(8,128)(2,1)S(1)} %all-to-all-done.2) | copy-start | bytes 4866052
  540.0 64.6 %copy-start.43 = (bf16[394,768]{1,0:T(8,128)(2,1)S(1)}, bf16[394,768]{1,0:T(8,128)(2,1)}, u32[]{:S(2)}) copy-start(bf16[394,768]{1,0:T(8,128)(2,1)} %copy-done.42) | copy-start | bytes 1815556
  540.0 65.5 %copy-start.1 = (s32[788]{0:T(1024)S(1)}, s32[788]{0:T(1024)}, u32[]{:S(2)}) copy-start(s32[788]{0:T(1024)} %copy-done) | copy-start | bytes 9460
  540.0 76.6 %all-to-all-start.3 = ((bf16[4,2,101376]{2,1,0:T(2,128)(2,1)}), bf16[4,2,101376]{2,1,0:T(2,128)(2,1)S(1)}, u32[]{:S(2)}, u32[]{:S(2)}) async-start(bf16[4,2,101376]{2,1,0:T(2,128)(2,1)} %reshape.1191), calls=%async_computation.3 | async-start | bytes 3244032 | tf_op jit(solution)/shard_map/all_to_all | solution.py:100
  544.1 111.1 %all-gather.26.cloned.1.call-start = ((), (), s32[]{:S(2)}) async-start(), calls=%async_computation.47 | async-start | bytes 1474560 | tf_op jit(solution)/shard_map/all_gather | solution.py:277
  604.6 11.6 copy-start.137
  616.6 11.9 copy-start.81
  659.0 59.2 %copy-start.45 = (bf16[394,768]{1,0:T(8,128)(2,1)}, bf16[394,768]{1,0:T(8,128)(2,1)S(1)}, u32[]{:S(2)}) copy-start(bf16[394,768]{1,0:T(8,128)(2,1)S(1)} %add_convert_fusion.1) | copy-start | bytes 1815556
  660.2 11.6 copy-start.185
  667.2 44.5 %copy-start.95 = (bf16[2,197,768]{2,0,1:T(2,128)(2,1)S(1)}, bf16[2,197,768]{2,0,1:T(2,128)(2,1)}, u32[]{:S(2)}) copy-start(bf16[2,197,768]{2,0,1:T(2,128)(2,1)} %param.21) | copy-start | bytes 1815556
  667.2 75.3 %all-to-all-start.4 = ((bf16[4,264,768]{2,1,0:T(8,128)(2,1)}), bf16[4,264,768]{2,1,0:T(8,128)(2,1)}, u32[]{:S(2)}, u32[]{:S(2)}) async-start(bf16[4,264,768]{2,1,0:T(8,128)(2,1)} %bitcast.26), calls=%async_computation.4 | async-start | bytes 3244032 | tf_op jit(solution)/shard_map/all_to_all | solution.py:88
  742.6 40.9 %all-to-all-start.6 = ((bf16[4,264,768]{2,1,0:T(8,128)(2,1)}), bf16[4,264,768]{2,1,0:T(8,128)(2,1)S(1)}, u32[]{:S(2)}, u32[]{:S(2)}) async-start(bf16[4,264,768]{2,1,0:T(8,128)(2,1)} %bitcast.440), calls=%async_computation.6 | async-start | bytes 3244032 | tf_op jit(solution)/shard_map/all_to_all | solution.py:158
  827.6 36.8 %all-to-all-start.7 = ((bf16[4,2,101376]{2,1,0:T(2,128)(2,1)}), bf16[4,2,101376]{2,1,0:T(2,128)(2,1)}, u32[]{:S(2)}, u32[]{:S(2)}) async-start(bf16[4,2,101376]{2,1,0:T(2,128)(2,1)} %reshape.1195), calls=%async_computation.7 | async-start | bytes 3244032 | tf_op jit(solution)/shard_map/all_to_all | solution.py:172
  864.4 36.7 %all-to-all-start.5 = ((bf16[4,2,101376]{2,1,0:T(2,128)(2,1)}), bf16[4,2,101376]{2,1,0:T(2,128)(2,1)}, u32[]{:S(2)}, u32[]{:S(2)}) async-start(bf16[4,2,101376]{2,1,0:T(2,128)(2,1)} %reshape.1193), calls=%async_computation.5 | async-start | bytes 3244032 | tf_op jit(solution)/shard_map/all_to_all | solution.py:100
  971.5 42.4 %all-to-all-start.8 = ((bf16[4,264,768]{2,1,0:T(8,128)(2,1)}), bf16[4,264,768]{2,1,0:T(8,128)(2,1)}, u32[]{:S(2)}, u32[]{:S(2)}) async-start(bf16[4,264,768]{2,1,0:T(8,128)(2,1)} %bitcast.438), calls=%async_computation.8 | async-start | bytes 3244032 | tf_op jit(solution)/shard_map/all_to_all | solution.py:158
  976.0 568.4 %reduce-scatter.80.cloned.1.call-start = ((), (), s32[]{:S(2)}) async-start(), calls=%async_computation.56 | async-start | bytes 245760
  977.0 568.3 %reduce-scatter.74.cloned.1.call-start = ((), (), s32[]{:S(2)}) async-start(), calls=%async_computation.53 | async-start | bytes 245760
  978.0 568.2 %reduce-scatter.68.cloned.1.call-start = ((), (), s32[]{:S(2)}) async-start(), calls=%async_computation.50 | async-start | bytes 245760
  981.9 565.2 %reduce-scatter.66.cloned.1.call-start = ((), (), s32[]{:S(2)}) async-start(), calls=%async_computation.49 | async-start | bytes 245760
  1058.1 43.4 %all-to-all-start.9 = ((bf16[4,2,101376]{2,1,0:T(2,128)(2,1)}), bf16[4,2,101376]{2,1,0:T(2,128)(2,1)S(1)}, u32[]{:S(2)}, u32[]{:S(2)}) async-start(bf16[4,2,101376]{2,1,0:T(2,128)(2,1)} %reshape.1197), calls=%async_computation.9 | async-start | bytes 3244032 | tf_op jit(solution)/shard_map/all_to_all | solution.py:172
  1061.7 486.3 %reduce-scatter.86.cloned.1.call-start = ((), (), s32[]{:S(2)}) async-start(), calls=%async_computation.59 | async-start | bytes 5308416
  1099.3 452.1 %reduce-scatter.78.cloned.1.call-start = ((), (), s32[]{:S(2)}) async-start(), calls=%async_computation.55 | async-start | bytes 245760
  1157.5 394.8 %reduce-scatter.72.cloned.1.call-start = ((), (), s32[]{:S(2)}) async-start(), calls=%async_computation.52 | async-start | bytes 245760
  1158.5 394.7 %reduce-scatter.64.cloned.1.call-start = ((), (), s32[]{:S(2)}) async-start(), calls=%async_computation.48 | async-start | bytes 245760
  1159.6 394.5 %reduce-scatter.56.cloned.1.call-start = ((), (), s32[]{:S(2)}) async-start(), calls=%async_computation.38 | async-start | bytes 1474560 | tf_op jit(solution)/shard_map/reduce_scatter | solution.py:318
  1162.8 391.3 %reduce-scatter.50.cloned.1.call-start = ((), (), s32[]{:S(2)}) async-start(), calls=%async_computation.35 | async-start | bytes 4423680 | tf_op jit(solution)/shard_map/reduce_scatter | solution.py:315
  1191.1 45.1 %all-to-all-start.10 = ((bf16[4,264,768]{2,1,0:T(8,128)(2,1)}), bf16[4,264,768]{2,1,0:T(8,128)(2,1)}, u32[]{:S(2)}, u32[]{:S(2)}) async-start(bf16[4,264,768]{2,1,0:T(8,128)(2,1)} %bitcast.439), calls=%async_computation.10 | async-start | bytes 3244032 | tf_op jit(solution)/shard_map/all_to_all | solution.py:158
  1195.5 358.7 %reduce-scatter.54.cloned.1.call-start = ((), (), s32[]{:S(2)}) async-start(), calls=%async_computation.37 | async-start | bytes 1474560 | tf_op jit(solution)/shard_map/reduce_scatter | solution.py:318
  1198.9 355.3 %reduce-scatter.48.cloned.1.call-start = ((), (), s32[]{:S(2)}) async-start(), calls=%async_computation.34 | async-start | bytes 4423680 | tf_op jit(solution)/shard_map/reduce_scatter | solution.py:315
  1282.7 81.1 %all-to-all-start.11 = ((bf16[4,2,101376]{2,1,0:T(2,128)(2,1)}), bf16[4,2,101376]{2,1,0:T(2,128)(2,1)S(1)}, u32[]{:S(2)}, u32[]{:S(2)}) async-start(bf16[4,2,101376]{2,1,0:T(2,128)(2,1)} %reshape.1199), calls=%async_computation.11 | async-start | bytes 3244032 | tf_op jit(solution)/shard_map/all_to_all | solution.py:172
  1286.2 267.9 %reduce-scatter.52.cloned.1.call-start = ((), (), s32[]{:S(2)}) async-start(), calls=%async_computation.36 | async-start | bytes 1474560 | tf_op jit(solution)/shard_map/reduce_scatter | solution.py:318
  1399.6 189.5 %reduce-scatter.46.cloned.1.call-start = ((), (), s32[]{:S(2)}) async-start(), calls=%async_computation.33 | async-start | bytes 4423680 | tf_op jit(solution)/shard_map/reduce_scatter | solution.py:315
  1422.8 223.7 %reduce-scatter.84.cloned.1.call-start = ((), (), s32[]{:S(2)}) async-start(), calls=%async_computation.58 | async-start | bytes 5308416
  1462.2 206.2 %reduce-scatter.76.cloned.1.call-start = ((), (), s32[]{:S(2)}) async-start(), calls=%async_computation.54 | async-start | bytes 245760
  1469.4 219.1 %reduce-scatter.70.cloned.1.call-start = ((), (), s32[]{:S(2)}) async-start(), calls=%async_computation.51 | async-start | bytes 245760
  1470.4 273.5 %reduce-scatter.82.cloned.1.call-start = ((), (), s32[]{:S(2)}) async-start(), calls=%async_computation.57 | async-start | bytes 5308416
  1508.3 292.8 %reduce-scatter.62.cloned.1.call-start = ((), (), s32[]{:S(2)}) async-start(), calls=%async_computation.41 | async-start | bytes 5308416 | tf_op jit(solution)/shard_map/reduce_scatter | solution.py:349
  1520.7 337.5 %reduce-scatter.60.cloned.1.call-start = ((), (), s32[]{:S(2)}) async-start(), calls=%async_computation.40 | async-start | bytes 5308416 | tf_op jit(solution)/shard_map/reduce_scatter | solution.py:349
  1531.4 383.9 %reduce-scatter.58.cloned.1.call-start = ((), (), s32[]{:S(2)}) async-start(), calls=%async_computation.39 | async-start | bytes 5308416 | tf_op jit(solution)/shard_map/reduce_scatter | solution.py:349
  1542.0 451.1 %all-reduce.5.cloned.1.call-start = ((), (), s32[]{:S(2)}) async-start(), calls=%async_computation.60 | async-start | bytes 7077888 | tf_op jit(solution)/shard_map/psum | solution.py:332
  1589.1 64.6 %copy-start.36 = (f32[394,768]{1,0:T(8,128)S(1)}, f32[394,768]{1,0:T(8,128)}, u32[]{:S(2)}) copy-start(f32[394,768]{1,0:T(8,128)} %copy-done.34) | copy-start | bytes 3631108
  (179 other events, 687.5 us)
Sparse Core Ops, SparseCore 0:
  10.7 72.6 all-gather.15
  85.5 28.8 all-gather.17
  133.3 91.8 all-gather.19
  276.4 52.2 all-gather.21
  405.4 89.2 all-gather.23
  546.7 48.1 all-gather.25
  979.1 36.1 reduce-scatter.79
  1017.5 36.0 reduce-scatter.73
  1055.9 22.5 reduce-scatter.67
  1080.5 31.8 reduce-scatter.65
  1116.5 60.8 reduce-scatter.85
  1179.5 19.6 reduce-scatter.77
  1201.4 27.3 reduce-scatter.71
  1230.8 26.7 reduce-scatter.63
  1260.4 28.7 reduce-scatter.55
  1291.9 84.9 reduce-scatter.49
  1379.0 42.9 reduce-scatter.53
  1424.8 65.0 reduce-scatter.47
  1492.2 29.4 reduce-scatter.51
  1523.9 65.0 reduce-scatter.45
  1592.5 53.9 reduce-scatter.83
  1648.7 19.5 reduce-scatter.75
  1670.6 17.8 reduce-scatter.69
  1691.8 51.9 reduce-scatter.81
  1747.3 53.7 reduce-scatter.61
  1804.4 53.7 reduce-scatter.59
  1861.5 53.7 reduce-scatter.57
  1919.2 73.8 all-reduce.4
where the time goes:
time: 2020 us; the launch traced here: 2010 us
  waiting for transfers between devices  758 us (38%)
  local copies, waits for them, and re-layouts  457 us (23%)
  matrix products  370 us (18%)
  blocking collectives  183 us (9%)
  other arithmetic  167 us (8%)
  starting transfers between devices  52.7 us (3%)
    unnamed x471, local copies, waits for them, and re-layouts  200 us
    reduce_scatter x3, waiting for transfers between devices, shards(): lax.psum_scatter(local_second.astype(jnp.bfloat16), 'replica', scatter_di...  168 us
    all_gather x3, blocking collectives, shards(): lax.all_gather(router_weight[layer_index], 'shard', axis=0, tiled=True)  160 us
    all_to_all x3, waiting for transfers between devices, forward_layer(): lax.all_to_all(buffer.reshape(experts, capacity, features), 'shard', spli...  137 us
    unnamed x40, waiting for transfers between devices  118 us
    dot_general x3, matrix products, forward_layer(): jnp.einsum('emd,edf->emf', arrived, first_weight, preferred_element_type=...  109 us
    all_to_all x3, waiting for transfers between devices, backward_layer(): lax.all_to_all(grad_rows, 'shard', split_axis=1, concat_axis=0, tiled=True)  78.9 us
    psum x1, waiting for transfers between devices, shards(): lax.psum(summed[0].astype(jnp.bfloat16), 'replica').astype(jnp.float32)  72.2 us
  transfers between devices with their start and end apart: 40, of which 18 were waited for; matrix products, arithmetic and copies ran while one was open for 41% of the time, Pallas kernels for 0%

commit v1 on v0

v1 whole, which is shorter than its diff:
```python
import jax
import jax.numpy as jnp
from jax import lax
from jax.sharding import PartitionSpec as P

HEAD = 64
LAYERS = 3

eps_norm = 1e-06
inv_root_two = 0.7071067811865476
inv_root_two_pi = 0.3989422804014327
bf16 = jnp.bfloat16
f32 = jnp.float32


def norm_parts(values_in):
    average = jnp.mean(values_in, axis=-1, keepdims=True)
    centred = values_in - average
    variance = jnp.mean(centred * centred, axis=-1, keepdims=True)
    inverse = lax.rsqrt(variance + eps_norm)
    return (centred * inverse, inverse)


def norm_back(grad_out, normed, inverse, gain_row):
    scaled = grad_out * gain_row
    inner = jnp.mean(scaled, axis=-1, keepdims=True)
    along = jnp.mean(scaled * normed, axis=-1, keepdims=True)
    grad_in = inverse * (scaled - inner - normed * along)
    return (grad_in, jnp.sum(grad_out * normed, axis=0), jnp.sum(grad_out, axis=0))


def dot_on(left, right, left_axis, right_axis):
    return lax.dot_general(
        left, right, (((left_axis,), (right_axis,)), ((), ())), preferred_element_type=f32
    )


def swap(values, bit):
    count = lax.axis_size("replica")
    return lax.ppermute(values, "replica", [(n, n ^ bit) for n in range(count)])


def bit_of(bit):
    return (lax.axis_index("replica") & bit) != 0


def orders():
    bits = []
    step = 2
    while step < lax.axis_size("replica"):
        bits.append(step)
        step *= 2
    return bits, bits[::-1]


def halve(values, bit, size):
    rows = values.shape[0]
    view = values.reshape((rows // (2 * size), 2, size) + values.shape[1:])
    own = bit_of(bit).astype(jnp.int32)
    kept = lax.dynamic_index_in_dim(view, own, 1, keepdims=False)
    sent = lax.dynamic_index_in_dim(view, 1 - own, 1, keepdims=False)
    return kept.reshape((rows // 2,) + values.shape[1:]), sent.reshape((rows // 2,) + values.shape[1:])


def scatter_replica(values):
    kept, sent = halve(values, 1, 1)
    values = (kept.astype(f32) + swap(sent, 1).astype(f32)).astype(bf16)
    middle = values.shape[-2] // 16 * 8
    parts = []
    for piece, order in zip((values[..., :middle, :], values[..., middle:, :]), orders()):
        for at, bit in enumerate(order):
            size = 1
            for other in order[at + 1 :]:
                if other < bit:
                    size *= 2
            kept, sent = halve(piece, bit, size)
            piece = (kept.astype(f32) + swap(sent, bit).astype(f32)).astype(bf16)
        parts.append(piece[0])
    return parts


def gather_replica(parts):
    done = []
    for piece, order in zip(parts, orders()):
        piece = piece[None]
        held = []
        for bit in order[::-1]:
            size = 1
            for other in held:
                if other < bit:
                    size *= 2
            other_piece = swap(piece, bit)
            rows = piece.shape[0]
            shape = (rows // size, size) + piece.shape[1:]
            mine, theirs = piece.reshape(shape), other_piece.reshape(shape)
            upper = bit_of(bit)
            piece = jnp.stack(
                [jnp.where(upper, theirs, mine), jnp.where(upper, mine, theirs)], axis=1
            ).reshape((2 * rows,) + piece.shape[1:])
            held.append(bit)
        done.append(piece)
    values = jnp.concatenate(done, axis=-2)
    other = swap(values, 1)
    upper = bit_of(1)
    rows = values.shape[0]
    return jnp.stack(
        [jnp.where(upper, other, values), jnp.where(upper, values, other)], axis=1
    ).reshape((2 * rows,) + values.shape[1:])


def gather_dense(packed):
    rows, columns = packed.shape
    count = lax.axis_size("replica")
    width = columns // count
    own = lax.dynamic_slice_in_dim(packed, lax.axis_index("replica") * width, width, axis=1)
    tall = lax.all_gather(own, "shard", axis=0, tiled=True)
    return lax.all_gather(tall, "replica", axis=0, tiled=False)


def reduce_dense(grad_qkv_w, grad_out_w, items):
    features = grad_out_w.shape[0]
    count = lax.axis_size("replica")
    shards_ = lax.axis_size("shard")
    rows = features // shards_
    dense = jnp.concatenate([grad_qkv_w.astype(bf16), grad_out_w.astype(bf16)], axis=1)
    width = dense.shape[1] // count
    chunks = jnp.transpose(dense.reshape(shards_, rows, count, width), (2, 0, 1, 3))
    extra = jnp.zeros((count, shards_, 8, width), bf16)
    small = items.astype(bf16).reshape(items.shape[0], shards_, rows)
    extra = extra.at[: items.shape[0], :, 0, :rows].set(small)
    chunks = jnp.concatenate([chunks, extra], axis=2)
    parts = scatter_replica(chunks)
    whole = jnp.concatenate(parts, axis=-2)
    swapped = lax.all_to_all(whole, "shard", split_axis=0, concat_axis=0, tiled=True)
    total = jnp.sum(swapped.astype(f32), axis=0).astype(bf16)
    middle = total.shape[-2] // 16 * 8
    result = gather_replica([total[:middle], total[middle:]])
    body = jnp.transpose(result[:, :rows], (1, 0, 2)).reshape(rows, count * width)
    return (
        body[:, : 3 * features].astype(f32),
        body[:, 3 * features :].astype(f32),
        result[: items.shape[0], rows, :rows].astype(f32),
    )


def split_heads(qkv_rows, images, length, head_count):
    features = qkv_rows.shape[1] // 3
    head_size = features // head_count
    queries = qkv_rows[:, :features].reshape(images, length, head_count, head_size)
    key_rows = qkv_rows[:, features : 2 * features].reshape(images, length, head_count, head_size)
    value_rows = qkv_rows[:, 2 * features :].reshape(images, length, head_count, head_size)
    return (queries, key_rows, value_rows)


def attend(queries, key_rows):
    scores = jnp.einsum(
        "bqhd,bkhd->bhqk", queries, key_rows, preferred_element_type=f32
    ) * queries.shape[-1] ** (-0.5)
    highest = jnp.max(scores, axis=-1, keepdims=True)
    raised = jnp.exp(scores - highest)
    row_total = jnp.sum(raised, axis=-1, keepdims=True)
    return (raised / row_total, highest + jnp.log(row_total))


def exchange(rows, experts):
    shape = rows.shape
    blocks = rows.reshape(experts, shape[0] // experts, shape[1])
    return lax.all_to_all(blocks, "shard", split_axis=0, concat_axis=0, tiled=True).reshape(shape)


def forward_layer(
    residual, qkv_w, out_w, router_t, gains, shifts, first_weight, second_weight, choose, places, info
):
    images, length, head_count, experts = info
    token_count, features = residual.shape
    normed_one, inverse_one = norm_parts(residual)
    hidden_one = (normed_one * gains[0] + shifts[0]).astype(bf16)
    qkv_rows = jnp.dot(hidden_one, qkv_w, preferred_element_type=f32).astype(bf16)
    queries, key_rows, value_rows = split_heads(qkv_rows, images, length, head_count)
    attn_weights, log_total = attend(queries, key_rows)
    context = (
        jnp.einsum(
            "bhqk,bkhd->bqhd", attn_weights.astype(bf16), value_rows, preferred_element_type=f32
        )
        .astype(bf16)
        .reshape(token_count, features)
    )
    middle = residual + jnp.dot(context, out_w, preferred_element_type=f32)
    normed_two, inverse_two = norm_parts(middle)
    hidden_two = (normed_two * gains[1] + shifts[1]).astype(bf16)
    router = jax.nn.softmax(dot_on(hidden_two, router_t, 1, 1), axis=-1)
    gates = [jnp.sum(choose[k] * router, axis=1, keepdims=True) for k in range(2)]
    both, singles = places
    arrived = exchange(dot_on(both, hidden_two, 0, 0).astype(bf16), experts)
    pre_act = jnp.dot(arrived, first_weight, preferred_element_type=f32)
    spread = lax.erf(pre_act * inv_root_two)
    activated = (0.5 * pre_act * (1.0 + spread)).astype(bf16)
    slope = (
        0.5 * (1.0 + spread) + pre_act * jnp.exp(-0.5 * pre_act * pre_act) * inv_root_two_pi
    ).astype(bf16)
    produced = jnp.dot(activated, second_weight, preferred_element_type=f32).astype(bf16)
    returned = exchange(produced, experts)
    picked = [jnp.dot(singles[k], returned, preferred_element_type=f32) for k in range(2)]
    residual_next = middle + (gates[0] * picked[0] + gates[1] * picked[1])
    picked = [p.astype(bf16) for p in picked]
    record = (
        normed_one, inverse_one, hidden_one, qkv_rows, log_total, context, normed_two, inverse_two,
        hidden_two, router, gates, arrived, slope, activated, picked,
    )
    return (record, residual_next)


def backward_layer(
    gradient, record, qkv_w, out_w, router_t, gains, first_weight, second_weight, choose, places, info
):
    images, length, head_count, experts = info
    (
        normed_one, inverse_one, hidden_one, qkv_rows, log_total, context, normed_two, inverse_two,
        hidden_two, router, gates, arrived, slope, activated, picked,
    ) = record
    both, singles = places
    token_count, features = gradient.shape
    grad_slots = dot_on(singles[0], (gates[0] * gradient).astype(bf16), 0, 0) + dot_on(
        singles[1], (gates[1] * gradient).astype(bf16), 0, 0
    )
    grad_arrived = exchange(grad_slots.astype(bf16), experts)
    grad_act = dot_on(grad_arrived, second_weight, 1, 1)
    grad_pre = (grad_act * slope.astype(f32)).astype(bf16)
    grad_rows = dot_on(grad_pre, first_weight, 1, 1).astype(bf16)
    grad_back = exchange(grad_rows, experts)
    expert_terms = jnp.concatenate(
        [dot_on(grad_pre, arrived, 0, 0).astype(bf16), dot_on(activated, grad_arrived, 0, 0).astype(bf16)],
        axis=1,
    )
    grad_router = sum(
        choose[k] * jnp.sum(gradient * picked[k].astype(f32), axis=1, keepdims=True) for k in range(2)
    )
    grad_logits = (
        router * (grad_router - jnp.sum(router * grad_router, axis=-1, keepdims=True))
    ).astype(bf16)
    grad_router_w = dot_on(grad_logits, hidden_two, 0, 0)
    grad_two = jnp.dot(both, grad_back, preferred_element_type=f32) + jnp.dot(
        grad_logits, router_t, preferred_element_type=f32
    )
    grad_norm_two, gain_two, shift_two = norm_back(grad_two, normed_two, inverse_two, gains[1])
    grad_middle = gradient + grad_norm_two
    grad_attn = grad_middle.astype(bf16)
    grad_out_w = dot_on(context, grad_attn, 0, 0)
    queries, key_rows, value_rows = split_heads(qkv_rows, images, length, head_count)
    grad_context = dot_on(grad_attn, out_w, 1, 1).astype(bf16).reshape(queries.shape)
    score_scale = queries.shape[-1] ** (-0.5)
    scores = (
        jnp.einsum("bqhd,bkhd->bhqk", queries, key_rows, preferred_element_type=f32) * score_scale
    )
    attn_weights = jnp.exp(scores - log_total)
    grad_weights = jnp.einsum(
        "bqhd,bkhd->bhqk", grad_context, value_rows, preferred_element_type=f32
    )
    grad_values = jnp.einsum(
        "bhqk,bqhd->bkhd", attn_weights.astype(bf16), grad_context, preferred_element_type=f32
    )
    grad_scores = (
        attn_weights * (grad_weights - jnp.sum(attn_weights * grad_weights, axis=-1, keepdims=True))
    ).astype(bf16)
    grad_queries = (
        jnp.einsum("bhqk,bkhd->bqhd", grad_scores, key_rows, preferred_element_type=f32) * score_scale
    )
    grad_keys = (
        jnp.einsum("bhqk,bqhd->bkhd", grad_scores, queries, preferred_element_type=f32) * score_scale
    )
    grad_qkv = jnp.concatenate(
        [
            grad_queries.reshape(token_count, features),
            grad_keys.reshape(token_count, features),
            grad_values.reshape(token_count, features),
        ],
        axis=1,
    ).astype(bf16)
    grad_qkv_w = dot_on(hidden_one, grad_qkv, 0, 0)
    grad_one = dot_on(grad_qkv, qkv_w, 1, 1)
    grad_norm_one, gain_one, shift_one = norm_back(grad_one, normed_one, inverse_one, gains[0])
    items = jnp.concatenate(
        [grad_router_w, jnp.stack([gain_one, gain_two, shift_one, shift_two])], axis=0
    )
    return (grad_middle + grad_norm_one, (grad_qkv_w, grad_out_w, items), expert_terms)


def shards(
    tokens, expert_ids, qkv_weight, out_weight, router_weight, norm_gain, norm_shift, expert_in,
    expert_out, cotangent,
):
    images, length, features = tokens.shape
    token_count = images * length
    head_count = features // HEAD
    experts = lax.axis_size("shard")
    capacity = (8 * token_count + 24 * experts - 1) // (24 * experts) * 8
    slots = experts * capacity
    packed = jnp.concatenate([qkv_weight, out_weight], axis=2)
    gathered = [gather_dense(packed[index]) for index in range(LAYERS)]
    router_all = lax.all_gather(
        jnp.transpose(router_weight, (0, 2, 1)).reshape(LAYERS * experts, -1), "shard", axis=1, tiled=True
    ).reshape(LAYERS, experts, features)
    ids_pair = expert_ids.reshape(token_count, 2)
    ids_flat = ids_pair.reshape(-1)
    labels = jnp.arange(experts, dtype=jnp.int32)
    member = (ids_flat[:, None] == labels[None, :]).astype(jnp.int32)
    earlier = jnp.cumsum(member, axis=0) - member
    positions = (ids_flat * capacity + jnp.sum(earlier * member, axis=1)).reshape(token_count, 2)
    choose = [(ids_pair[:, k : k + 1] == labels[None, :]).astype(f32) for k in range(2)]
    slot_row = jnp.arange(slots, dtype=jnp.int32)[None, :]
    singles = [(positions[:, k : k + 1] == slot_row).astype(bf16) for k in range(2)]
    places = (singles[0] + singles[1], singles)
    info = (images, length, head_count, experts)
    residual = tokens.reshape(token_count, features).astype(f32)
    records = []
    weights = []
    for index in range(LAYERS):
        whole = jnp.transpose(gathered[index], (1, 0, 2)).reshape(features, 4 * features)
        dense_set = (whole[:, : 3 * features], whole[:, 3 * features :], router_all[index])
        weights.append(dense_set)
        record, residual = forward_layer(
            residual, *dense_set, norm_gain[index], norm_shift[index], expert_in[index, 0],
            expert_out[index, 0], choose, places, info,
        )
        records.append(record)
    activations = residual.astype(bf16).reshape(images, length, features)
    gradient = cotangent.reshape(token_count, features).astype(f32)
    dense_out = [None] * LAYERS
    expert_sums = [None] * LAYERS
    for index in range(LAYERS - 1, -1, -1):
        gradient, dense_terms, expert_terms = backward_layer(
            gradient, records[index], *weights[index], norm_gain[index], expert_in[index, 0],
            expert_out[index, 0], choose, places, info,
        )
        expert_sums[index] = lax.psum_scatter(
            expert_terms, "replica", scatter_dimension=0, tiled=True
        )
        dense_out[index] = reduce_dense(*dense_terms)
    input_grad = gradient.reshape(images, length, features)
    qkv_grad = jnp.stack([dense_out[index][0] for index in range(LAYERS)])
    out_grad = jnp.stack([dense_out[index][1] for index in range(LAYERS)])
    items = jnp.stack([dense_out[index][2] for index in range(LAYERS)])
    router_grad = jnp.transpose(items[:, :experts], (0, 2, 1))
    gain_grad = items[:, experts : experts + 2]
    shift_grad = items[:, experts + 2 :]
    expert_in_grad = jnp.stack(
        [jnp.transpose(expert_sums[index][:, :features].astype(f32))[None] for index in range(LAYERS)]
    )
    expert_out_grad = jnp.stack(
        [expert_sums[index][:, features:].astype(f32)[None] for index in range(LAYERS)]
    )
    return (
        activations, input_grad, qkv_grad, out_grad, router_grad, gain_grad, shift_grad,
        expert_in_grad, expert_out_grad,
    )


def solution(mesh):
    in_specs = (
        P(("replica", "shard"), None, None),
        P(("replica", "shard"), None, None),
        P(None, "shard", None),
        P(None, "shard", None),
        P(None, "shard", None),
        P(),
        P(),
        P(None, "shard", None, None),
        P(None, "shard", None, None),
        P(("replica", "shard"), None, None),
    )
    out_specs = (
        P(("replica", "shard"), None, None),
        P(("replica", "shard"), None, None),
        P(None, "shard", None),
        P(None, "shard", None),
        P(None, "shard", None),
        P(None, None, "shard"),
        P(None, None, "shard"),
        P(None, "shard", None, "replica"),
        P(None, "shard", "replica", None),
    )
    return jax.shard_map(shards, mesh=mesh, in_specs=in_specs, out_specs=out_specs, check_vma=False)
```

time: 2020 us -> 1210 us (0.60)
  waiting for transfers between devices: 758 us -> 230 us
  local copies, waits for them, and re-layouts: 457 us -> 244 us
  other arithmetic: 167 us -> 93.8 us
  matrix products: 370 us -> 329 us
  starting transfers between devices: 52.7 us -> 91.9 us
    reduce_scatter x9 -> x0, waiting for transfers between devices: 203 us -> none  [the longest x3 168 us: shards(): lax.psum_scatter(local_second.astype(jnp.bfloat16), 'replica', scatter_di...]
    all_to_all x12 -> x14, waiting for transfers between devices: 291 us -> 128 us  [the longest x11 120 us: exchange(): lax.all_to_all(blocks, 'shard', split_axis=0, concat_axis=0, tiled=True)]
    unnamed x471 -> x406, local copies, waits for them, and re-layouts: 200 us -> 79 us
    unnamed x40 -> x9, waiting for transfers between devices: 118 us -> 0.11 us
    psum x1 -> x0, waiting for transfers between devices: 72.2 us -> none  [shards(): lax.psum(summed[0].astype(jnp.bfloat16), 'replica').astype(jnp.float32)]
    convert_element_type x19 -> x7, local copies, waits for them, and re-layouts: 77.8 us -> 9.62 us  [the longest x2 4.67 us: shards(): gradient = cotangent.reshape(token_count, features).astype(f32)]
    unnamed x9 -> x7, other arithmetic: 63.5 us -> 0.08 us
    gather x17 -> x0, local copies, waits for them, and re-layouts: 56.7 us -> none  [the longest x11 32.9 us: forward_layer(): gate_values = jnp.take_along_axis(router, ids_pair, axis=1)]
  transfers between devices with their start and end apart: 40 -> 50, of which waited for: 18 -> 31; matrix products, arithmetic and copies ran while one was open for 41% -> 39% of each run, Pallas kernels for 0% -> 0%
where the time goes in v1:
time: 1210 us; the launch traced here: 1200 us
  matrix products  329 us (27%)
  local copies, waits for them, and re-layouts  244 us (20%)
  waiting for transfers between devices  230 us (19%)
  blocking collectives  194 us (16%)
  other arithmetic  93.8 us (8%)
  starting transfers between devices  91.9 us (8%)
  between operations  17.9 us (1%)
    dot_general x39, matrix products, dot_on(): lax.dot_general(left, right, (((left_axis,), (right_axis,)), ((), ())), p...  179 us
    all_to_all x11, waiting for transfers between devices, exchange(): lax.all_to_all(blocks, 'shard', split_axis=0, concat_axis=0, tiled=True)  120 us
    all_gather x3, blocking collectives, gather_dense(): tall = lax.all_gather(own, 'shard', axis=0, tiled=True)  114 us
    unnamed x406, local copies, waits for them, and re-layouts  79 us
    ppermute x30, waiting for transfers between devices, swap(): return lax.ppermute(values, 'replica', [(n, n ^ bit) for n in range(count)])  56.7 us
    all_to_all x11, starting transfers between devices, exchange(): lax.all_to_all(blocks, 'shard', split_axis=0, concat_axis=0, tiled=True)  48.7 us
    all_gather x3, waiting for transfers between devices, gather_dense(): return lax.all_gather(tall, 'replica', axis=0, tiled=False)  45.2 us
    all_gather x1, blocking collectives, shards(): lax.all_gather(jnp.transpose(router_weight, (0, 2, 1)).reshape(LAYERS * e...  40.1 us
  transfers between devices with their start and end apart: 50, of which 31 were waited for; matrix products, arithmetic and copies ran while one was open for 39% of the time, Pallas kernels for 0%

profile of v1, /device:TPU:0, one launch (start us, length us, event | category | flops | bytes accessed | tf_op | source)
XLA Modules:
  0.0 1200.1 jit_solution(13812563657526898915)
XLA Ops:
  11.2 18.6 %all-gather = bf16[1,768,384]{2,1,0:T(8,128)(2,1)} all-gather(bf16[1,192,384]{2,1,0:T(8,128)(2,1)S(1)} %constant_dynamic-slice_fusion.8), channel_id=2, replica_groups=mesh['replica'=8,'shard'=4] {'shard'}, dimensions={1}, use_global_device_ids=true | all-gather | bytes 737280 | tf_op jit(solution)/shard_map/all_gather | solution.py:116
  37.6 32.8 %all-gather.11.cloned.1.call-done = bf16[8,768,384]{2,1,0:T(8,128)(2,1)} async-done(((bf16[1,768,384]{2,1,0:T(8,128)(2,1)}), bf16[8,768,384]{2,1,0:T(8,128)(2,1)}) %all-gather.11.cloned.1.call-update) | async-done | bytes 4718608 | tf_op jit(solution)/shard_map/all_gather | solution.py:117
  70.4 6.6 copy.726
  107.9 4.6 all-to-all-start
  113.5 49.2 %all-gather.2 = bf16[1,768,384]{2,1,0:T(8,128)(2,1)} all-gather(bf16[1,192,384]{2,1,0:T(8,128)(2,1)S(1)} %constant_dynamic-slice_fusion.7), channel_id=4, replica_groups=mesh['replica'=8,'shard'=4] {'shard'}, dimensions={1}, use_global_device_ids=true | all-gather | bytes 737280 | tf_op jit(solution)/shard_map/all_gather | solution.py:116
  162.7 10.7 multiply_convert_fusion.2
  173.4 11.0 fusion.66
  184.4 4.8 all-to-all-start.1
  189.2 40.1 %all-gather.6 = bf16[4,192,12]{1,2,0:T(8,128)(2,1)S(1)} all-gather(bf16[1,192,12]{1,2,0:T(8,128)(2,1)S(1)} %bitcast.681), channel_id=1, replica_groups=mesh['replica'=8,'shard'=4] {'shard'}, dimensions={0}, use_global_device_ids=true | all-gather | bytes 23040 | tf_op jit(solution)/shard_map/all_gather | solution.py:300
  229.5 6.8 copy.739
  277.6 46.2 %all-gather.4 = bf16[1,768,384]{2,1,0:T(8,128)(2,1)} all-gather(bf16[1,192,384]{2,1,0:T(8,128)(2,1)S(1)} %constant_dynamic-slice_fusion.6), channel_id=6, replica_groups=mesh['replica'=8,'shard'=4] {'shard'}, dimensions={1}, use_global_device_ids=true | all-gather | bytes 737280 | tf_op jit(solution)/shard_map/all_gather | solution.py:116
  323.9 10.9 multiply_convert_fusion.1
  334.8 11.0 fusion.72
  345.7 4.8 all-to-all-start.3
  350.6 12.3 %all-gather.15.cloned.1.call-done = bf16[8,768,384]{2,1,0:T(8,128)(2,1)} async-done(((bf16[1,768,384]{2,1,0:T(8,128)(2,1)}), bf16[8,768,384]{2,1,0:T(8,128)(2,1)}) %all-gather.15.cloned.1.call-update) | async-done | bytes 4718608 | tf_op jit(solution)/shard_map/all_gather | solution.py:117
  362.9 6.7 copy.748
  371.2 13.3 %all-to-all-done.3 = bf16[4,264,768]{2,1,0:T(8,128)(2,1)S(1)} async-done(((bf16[4,264,768]{2,1,0:T(8,128)(2,1)}), bf16[4,264,768]{2,1,0:T(8,128)(2,1)S(1)}, u32[]{:S(2)}, u32[]{:S(2)}) %all-to-all-start.3) | async-done | bytes 1622048 | tf_op jit(solution)/shard_map/all_to_all | solution.py:168
  419.1 39.9 %all_to_all.75 = bf16[4,264,768]{2,1,0:T(8,128)(2,1)S(1)} all-to-all(bf16[4,264,768]{2,1,0:T(8,128)(2,1)S(1)} %bitcast.651), channel_id=1, replica_groups=mesh['replica'=8,'shard'=4] {'shard'}, dimensions={0} | all-to-all | bytes 3244032 | tf_op jit(solution)/shard_map/all_to_all | solution.py:168
  459.0 10.7 multiply_convert_fusion
  469.6 11.0 fusion.78
  480.6 4.8 all-to-all-start.5
  491.4 31.3 %all-to-all-done.5 = bf16[4,264,768]{2,1,0:T(8,128)(2,1)} async-done(((bf16[4,264,768]{2,1,0:T(8,128)(2,1)}), bf16[4,264,768]{2,1,0:T(8,128)(2,1)}, u32[]{:S(2)}, u32[]{:S(2)}) %all-to-all-start.5) | async-done | bytes 1622048 | tf_op jit(solution)/shard_map/all_to_all | solution.py:168
  525.3 4.1 multiply_reduce_fusion.23
  533.4 4.5 all-to-all-start.6
  542.0 33.5 %all-to-all-done.6 = bf16[4,264,768]{2,1,0:T(8,128)(2,1)} async-done(((bf16[4,264,768]{2,1,0:T(8,128)(2,1)}), bf16[4,264,768]{2,1,0:T(8,128)(2,1)}, u32[]{:S(2)}, u32[]{:S(2)}) %all-to-all-start.6) | async-done | bytes 1622048 | tf_op jit(solution)/shard_map/all_to_all | solution.py:168
  575.5 11.0 convolution_convert_fusion
  586.5 11.2 fusion.15
  597.7 11.1 fusion.75
  608.9 4.3 all-to-all-start.7
  613.3 9.9 convolution_convert_fusion.1
  623.2 9.9 pad_maximum_fusion.2
  633.1 12.6 %copy.852 = bf16[3072,1536]{1,0:T(8,128)(2,1)} copy(bf16[3072,1536]{0,1:T(8,128)(2,1)} %pad_maximum_fusion.2) | data formatting | bytes 18874368
  645.7 5.1 all-to-all-done.7
  650.8 4.1 multiply_reduce_fusion.6
  696.5 5.0 multiply_reduce_fusion.7
  706.3 4.7 all-to-all-start.8
  711.4 4.1 convolution_convert_fusion.6
  730.4 17.9 %all-to-all-done.8 = bf16[4,264,768]{2,1,0:T(8,128)(2,1)} async-done(((bf16[4,264,768]{2,1,0:T(8,128)(2,1)}), bf16[4,264,768]{2,1,0:T(8,128)(2,1)}, u32[]{:S(2)}, u32[]{:S(2)}) %all-to-all-start.8) | async-done | bytes 1622048 | tf_op jit(solution)/shard_map/all_to_all | solution.py:168
  748.3 11.3 fusion.16
  759.7 4.1 fusion.24
  767.4 8.7 fusion.69
  782.6 9.9 convolution_convert_fusion.2
  797.0 10.8 convolution_convert_fusion.3
  814.8 9.2 pad_maximum_fusion.1
  824.0 12.7 %copy.850 = bf16[3072,1536]{1,0:T(8,128)(2,1)} copy(bf16[3072,1536]{0,1:T(8,128)(2,1)} %pad_maximum_fusion.1) | data formatting | bytes 18874368
  888.8 4.7 multiply_reduce_fusion.9
  893.5 4.1 convolution_convert_fusion.7
  904.6 4.6 all-to-all-start.10
  915.8 5.2 fusion.22
  928.6 18.7 %all-to-all-done.10 = bf16[4,264,768]{2,1,0:T(8,128)(2,1)} async-done(((bf16[4,264,768]{2,1,0:T(8,128)(2,1)}), bf16[4,264,768]{2,1,0:T(8,128)(2,1)}, u32[]{:S(2)}, u32[]{:S(2)}) %all-to-all-start.10) | async-done | bytes 1622048 | tf_op jit(solution)/shard_map/all_to_all | solution.py:168
  947.3 11.2 fusion.17
  958.5 11.1 fusion.63
  969.6 4.4 all-to-all-start.11
  974.4 9.7 convolution_convert_fusion.4
  990.3 6.9 convolution_convert_fusion.5
  997.2 5.0 collective-permute-done.11
  1006.6 4.2 pad_maximum_fusion
  1010.8 12.7 %copy.848 = bf16[3072,1536]{1,0:T(8,128)(2,1)} copy(bf16[3072,1536]{0,1:T(8,128)(2,1)} %pad_maximum_fusion) | data formatting | bytes 18874368
  1024.7 5.1 all-to-all-start.13
  1085.9 3.9 collective-permute-done.15
  1092.7 6.6 collective-permute-done.16
  1109.1 10.7 collective-permute-done.1
  1131.1 5.9 all-to-all-start.12
  1144.8 4.0 all-to-all-done.12
  (825 shorter events, 435.7 us)
Async XLA Ops:
  7.2 63.3 %all-gather.11.cloned.1.call-start = ((), (), s32[]{:S(2)}) async-start(), calls=%async_computation.18 | async-start | bytes 5308416 | tf_op jit(solution)/shard_map/all_gather | solution.py:117
  32.5 69.9 %copy-start.13 = (f32[394,768]{1,0:T(8,128)}, f32[394,768]{1,0:T(8,128)S(1)}, u32[]{:S(2)}) copy-start(f32[394,768]{1,0:T(8,128)S(1)} %reshape.1292) | copy-start | bytes 3631108
  34.5 42.6 %copy-start.143 = (f32[394]{0:T(512)}, f32[394]{0:T(512)S(1)}, u32[]{:S(2)}) copy-start(f32[394]{0:T(512)S(1)} %rsqrt.52) | copy-start | bytes 4732
  34.6 42.5 %copy-start.145 = (f32[394]{0:T(512)}, f32[394]{0:T(512)S(1)}, u32[]{:S(2)}) copy-start(f32[394]{0:T(512)S(1)} %div.123) | copy-start | bytes 4732
  37.6 39.5 %copy-start.135 = (f32[768]{0:T(1024)}, f32[768]{0:T(1024)S(1)}, u32[]{:S(2)}) copy-start(f32[768]{0:T(1024)S(1)} %get-tuple-element.271) | copy-start | bytes 9220
  37.6 39.5 %copy-start.153 = (f32[768]{0:T(1024)}, f32[768]{0:T(1024)S(1)}, u32[]{:S(2)}) copy-start(f32[768]{0:T(1024)S(1)} %get-tuple-element.157) | copy-start | bytes 9220
  37.6 67.7 %copy-start.109 = (f32[768]{0:T(1024)}, f32[768]{0:T(1024)S(1)}, u32[]{:S(2)}) copy-start(f32[768]{0:T(1024)S(1)} %get-tuple-element.272) | copy-start | bytes 9220
  37.6 67.9 %copy-start.147 = (s32[394,1]{0,1:T(1,128)}, s32[394,1]{0,1:T(1,128)S(1)}, u32[]{:S(2)}) copy-start(s32[394,1]{0,1:T(1,128)S(1)} %get-tuple-element.229) | copy-start | bytes 4732
  37.6 200.9 %copy-start.123 = (s32[394,1]{0,1:T(1,128)}, s32[394,1]{0,1:T(1,128)S(1)}, u32[]{:S(2)}) copy-start(s32[394,1]{0,1:T(1,128)S(1)} %get-tuple-element.230) | copy-start | bytes 4732
  104.9 133.6 %copy-start.3 = (f32[394,768]{1,0:T(8,128)}, f32[394,768]{1,0:T(8,128)S(1)}, u32[]{:S(2)}) copy-start(f32[394,768]{1,0:T(8,128)S(1)} %get-tuple-element.234) | copy-start | bytes 3631108
  105.5 130.8 %copy-start.31 = (bf16[394,768]{1,0:T(8,128)(2,1)}, bf16[394,768]{1,0:T(8,128)(2,1)S(1)}, u32[]{:S(2)}) copy-start(bf16[394,768]{1,0:T(8,128)(2,1)S(1)} %add_convert_fusion.5) | copy-start | bytes 1815556
  107.9 54.7 %all-to-all-start = ((bf16[4,264,768]{2,1,0:T(8,128)(2,1)}), bf16[4,264,768]{2,1,0:T(8,128)(2,1)S(1)}, u32[]{:S(2)}, u32[]{:S(2)}) async-start(bf16[4,264,768]{2,1,0:T(8,128)(2,1)} %bitcast.649), calls=%async_computation | async-start | bytes 3244032 | tf_op jit(solution)/shard_map/all_to_all | solution.py:168
  112.5 116.9 %all-gather.13.cloned.1.call-start = ((), (), s32[]{:S(2)}) async-start(), calls=%async_computation.19 | async-start | bytes 5308416 | tf_op jit(solution)/shard_map/all_gather | solution.py:117
  184.4 53.0 %all-to-all-start.1 = ((bf16[4,264,768]{2,1,0:T(8,128)(2,1)}), bf16[4,264,768]{2,1,0:T(8,128)(2,1)S(1)}, u32[]{:S(2)}, u32[]{:S(2)}) async-start(bf16[4,264,768]{2,1,0:T(8,128)(2,1)} %bitcast.645), calls=%async_computation.1 | async-start | bytes 3244032 | tf_op jit(solution)/shard_map/all_to_all | solution.py:168
  229.4 499.6 %copy-start.92 = (bf16[768,12]{0,1:T(8,128)(2,1)}, bf16[768,12]{0,1:T(8,128)(2,1)S(1)}, u32[]{:S(2)}) copy-start(bf16[768,12]{0,1:T(8,128)(2,1)S(1)} %reshape.1311) | copy-start | bytes 55300
  269.3 117.0 %copy-start.5 = (f32[394,768]{1,0:T(8,128)}, f32[394,768]{1,0:T(8,128)S(1)}, u32[]{:S(2)}) copy-start(f32[394,768]{1,0:T(8,128)S(1)} %get-tuple-element.243) | copy-start | bytes 3631108
  270.6 99.0 %copy-start.33 = (bf16[394,768]{1,0:T(8,128)(2,1)}, bf16[394,768]{1,0:T(8,128)(2,1)S(1)}, u32[]{:S(2)}) copy-start(bf16[394,768]{1,0:T(8,128)(2,1)S(1)} %add_convert_fusion.3) | copy-start | bytes 1815556
  273.0 50.9 %all-to-all-start.2 = ((bf16[4,264,768]{2,1,0:T(8,128)(2,1)}), bf16[4,264,768]{2,1,0:T(8,128)(2,1)S(1)}, u32[]{:S(2)}, u32[]{:S(2)}) async-start(bf16[4,264,768]{2,1,0:T(8,128)(2,1)} %bitcast.648), calls=%async_computation.2 | async-start | bytes 3244032 | tf_op jit(solution)/shard_map/all_to_all | solution.py:168
  276.7 86.2 %all-gather.15.cloned.1.call-start = ((), (), s32[]{:S(2)}) async-start(), calls=%async_computation.20 | async-start | bytes 5308416 | tf_op jit(solution)/shard_map/all_gather | solution.py:117
  345.7 38.8 %all-to-all-start.3 = ((bf16[4,264,768]{2,1,0:T(8,128)(2,1)}), bf16[4,264,768]{2,1,0:T(8,128)(2,1)S(1)}, u32[]{:S(2)}, u32[]{:S(2)}) async-start(bf16[4,264,768]{2,1,0:T(8,128)(2,1)} %bitcast.646), calls=%async_computation.3 | async-start | bytes 3244032 | tf_op jit(solution)/shard_map/all_to_all | solution.py:168
  480.6 42.1 %all-to-all-start.5 = ((bf16[4,264,768]{2,1,0:T(8,128)(2,1)}), bf16[4,264,768]{2,1,0:T(8,128)(2,1)}, u32[]{:S(2)}, u32[]{:S(2)}) async-start(bf16[4,264,768]{2,1,0:T(8,128)(2,1)} %bitcast.650), calls=%async_computation.5 | async-start | bytes 3244032 | tf_op jit(solution)/shard_map/all_to_all | solution.py:168
  533.4 42.1 %all-to-all-start.6 = ((bf16[4,264,768]{2,1,0:T(8,128)(2,1)}), bf16[4,264,768]{2,1,0:T(8,128)(2,1)}, u32[]{:S(2)}, u32[]{:S(2)}) async-start(bf16[4,264,768]{2,1,0:T(8,128)(2,1)} %bitcast.643), calls=%async_computation.6 | async-start | bytes 3244032 | tf_op jit(solution)/shard_map/all_to_all | solution.py:168
  608.9 42.0 %all-to-all-start.7 = ((bf16[4,264,768]{2,1,0:T(8,128)(2,1)}), bf16[4,264,768]{2,1,0:T(8,128)(2,1)}, u32[]{:S(2)}, u32[]{:S(2)}) async-start(bf16[4,264,768]{2,1,0:T(8,128)(2,1)} %bitcast.647), calls=%async_computation.7 | async-start | bytes 3244032 | tf_op jit(solution)/shard_map/all_to_all | solution.py:168
  613.2 552.7 %reduce-scatter.14.cloned.1.call-start = ((), (), s32[]{:S(2)}) async-start(), calls=%async_computation.23 | async-start | bytes 10616832
  706.3 42.0 %all-to-all-start.8 = ((bf16[4,264,768]{2,1,0:T(8,128)(2,1)}), bf16[4,264,768]{2,1,0:T(8,128)(2,1)}, u32[]{:S(2)}, u32[]{:S(2)}) async-start(bf16[4,264,768]{2,1,0:T(8,128)(2,1)} %bitcast.644), calls=%async_computation.8 | async-start | bytes 3244032 | tf_op jit(solution)/shard_map/all_to_all | solution.py:168
  725.9 33.8 %collective-permute-start.20 = (bf16[4,4,200,384]{3,2,1,0:T(8,128)(2,1)S(1)}, bf16[4,4,200,384]{3,2,1,0:T(8,128)(2,1)}, u32[]{:S(2)}, u32[]{:S(2)}) collective-permute-start(bf16[4,4,200,384]{3,2,1,0:T(8,128)(2,1)S(1)} %dynamic-slice_bitcast_fusion), channel_id=1, source_target_pairs={{0,4},{4,0},{8,12},{12,8},{16,20},{20,16},{24,28},{28,24},{1,5},{5... | collective-permute-start | bytes 7372808 | tf_op jit(solution)/shard_map/ppermute | solution.py:40
  729.0 30.7 %slice-start.6 = ((s8[4915200]{0:T(1024)(128)(4,1)}), s8[720896]{0:T(1024)(128)(4,1)S(1)}, s32[]{:S(2)}) async-start(s8[4915200]{0:T(1024)(128)(4,1)} %bitcast.561), calls=%async_computation.30 | async-start | bytes 1441792
  764.2 14.4 %collective-permute-start.21 = (bf16[2,4,96,384]{3,2,1,0:T(8,128)(2,1)S(1)}, bf16[2,4,96,384]{3,2,1,0:T(8,128)(2,1)S(1)}, u32[]{:S(2)}, u32[]{:S(2)}) collective-permute-start(bf16[2,4,96,384]{3,2,1,0:T(8,128)(2,1)S(1)} %dynamic-slice_bitcast_fusion.6), channel_id=1, source_target_pairs={{0,8},{4,12},{8,0},{12,4},{16,24},{20,28},{24,16},{28,20},{1,9},{5... | collective-permute-start | bytes 1769480 | tf_op jit(solution)/shard_map/ppermute | solution.py:40
  765.8 16.5 %collective-permute-start.23 = (bf16[2,4,104,384]{3,2,1,0:T(8,128)(2,1)S(1)}, bf16[2,4,104,384]{3,2,1,0:T(8,128)(2,1)S(1)}, u32[]{:S(2)}, u32[]{:S(2)}) collective-permute-start(bf16[2,4,104,384]{3,2,1,0:T(8,128)(2,1)S(1)} %dynamic-slice_bitcast_fusion.3), channel_id=1, source_target_pairs={{0,16},{4,20},{8,24},{12,28},{16,0},{20,4},{24,8},{28,12},{1,17},{... | collective-permute-start | bytes 1916936 | tf_op jit(solution)/shard_map/ppermute | solution.py:40
  778.8 13.6 %collective-permute-start.22 = (bf16[1,4,96,384]{3,2,1,0:T(8,128)(2,1)S(1)}, bf16[1,4,96,384]{3,2,1,0:T(8,128)(2,1)S(1)}, u32[]{:S(2)}, u32[]{:S(2)}) collective-permute-start(bf16[1,4,96,384]{3,2,1,0:T(8,128)(2,1)S(1)} %constant_dynamic-slice_fusion.1), channel_id=1, source_target_pairs={{0,16},{4,20},{8,24},{12,28},{16,0},{20,4},{24,8},{28,12},{1,17},{... | collective-permute-start | bytes 884744 | tf_op jit(solution)/shard_map/ppermute | solution.py:40
  782.5 10.1 collective-permute-start.24
  793.5 17.6 %all-to-all-start.14 = ((bf16[4,200,384]{2,1,0:T(8,128)(2,1)}), bf16[4,200,384]{2,1,0:T(8,128)(2,1)S(1)}, u32[]{:S(2)}, u32[]{:S(2)}) async-start(bf16[4,200,384]{2,1,0:T(8,128)(2,1)} %pad_maximum_fusion.13), calls=%async_computation.14 | async-start | bytes 1228800 | tf_op jit(solution)/shard_map/all_to_all | solution.py:134
  811.2 39.8 %all-to-all-start.9 = ((bf16[4,264,768]{2,1,0:T(8,128)(2,1)}), bf16[4,264,768]{2,1,0:T(8,128)(2,1)S(1)}, u32[]{:S(2)}, u32[]{:S(2)}) async-start(bf16[4,264,768]{2,1,0:T(8,128)(2,1)} %bitcast.637), calls=%async_computation.9 | async-start | bytes 3244032 | tf_op jit(solution)/shard_map/all_to_all | solution.py:168
  814.7 362.3 %reduce-scatter.12.cloned.1.call-start = ((), (), s32[]{:S(2)}) async-start(), calls=%async_computation.22 | async-start | bytes 10616832
  836.8 4.6 collective-permute-start.25
  838.1 5.3 collective-permute-start.27
  841.5 5.2 collective-permute-start.26
  843.4 5.3 collective-permute-start.28
  850.5 74.4 %collective-permute-start.29 = (bf16[4,200,384]{2,1,0:T(8,128)(2,1)}, bf16[4,200,384]{2,1,0:T(8,128)(2,1)}, u32[]{:S(2)}, u32[]{:S(2)}) collective-permute-start(bf16[4,200,384]{2,1,0:T(8,128)(2,1)} %pad_maximum_fusion.14), channel_id=1, source_target_pairs={{0,4},{4,0},{8,12},{12,8},{16,20},{20,16},{24,28},{28,24},{1,5},{5... | collective-permute-start | bytes 1843208 | tf_op jit(solution)/shard_map/ppermute | solution.py:40
  904.6 42.6 %all-to-all-start.10 = ((bf16[4,264,768]{2,1,0:T(8,128)(2,1)}), bf16[4,264,768]{2,1,0:T(8,128)(2,1)}, u32[]{:S(2)}, u32[]{:S(2)}) async-start(bf16[4,264,768]{2,1,0:T(8,128)(2,1)} %bitcast.641), calls=%async_computation.10 | async-start | bytes 3244032 | tf_op jit(solution)/shard_map/all_to_all | solution.py:168
  923.3 60.8 %collective-permute-start.10 = (bf16[4,4,200,384]{3,2,1,0:T(8,128)(2,1)S(1)}, bf16[4,4,200,384]{3,2,1,0:T(8,128)(2,1)}, u32[]{:S(2)}, u32[]{:S(2)}) collective-permute-start(bf16[4,4,200,384]{3,2,1,0:T(8,128)(2,1)S(1)} %dynamic-slice_bitcast_fusion.1), channel_id=1, source_target_pairs={{0,4},{4,0},{8,12},{12,8},{16,20},{20,16},{24,28},{28,24},{1,5},{5... | collective-permute-start | bytes 7372808 | tf_op jit(solution)/shard_map/ppermute | solution.py:40
  969.6 55.1 %all-to-all-start.11 = ((bf16[4,264,768]{2,1,0:T(8,128)(2,1)}), bf16[4,264,768]{2,1,0:T(8,128)(2,1)}, u32[]{:S(2)}, u32[]{:S(2)}) async-start(bf16[4,264,768]{2,1,0:T(8,128)(2,1)} %bitcast.642), calls=%async_computation.11 | async-start | bytes 3244032 | tf_op jit(solution)/shard_map/all_to_all | solution.py:168
  973.9 206.5 %reduce-scatter.10.cloned.1.call-start = ((), (), s32[]{:S(2)}) async-start(), calls=%async_computation.21 | async-start | bytes 10616832
  987.7 14.4 %collective-permute-start.11 = (bf16[2,4,96,384]{3,2,1,0:T(8,128)(2,1)S(1)}, bf16[2,4,96,384]{3,2,1,0:T(8,128)(2,1)S(1)}, u32[]{:S(2)}, u32[]{:S(2)}) collective-permute-start(bf16[2,4,96,384]{3,2,1,0:T(8,128)(2,1)S(1)} %dynamic-slice_bitcast_fusion.7), channel_id=1, source_target_pairs={{0,8},{4,12},{8,0},{12,4},{16,24},{20,28},{24,16},{28,20},{1,9},{5... | collective-permute-start | bytes 1769480 | tf_op jit(solution)/shard_map/ppermute | solution.py:40
  989.1 16.0 %collective-permute-start.13 = (bf16[2,4,104,384]{3,2,1,0:T(8,128)(2,1)S(1)}, bf16[2,4,104,384]{3,2,1,0:T(8,128)(2,1)S(1)}, u32[]{:S(2)}, u32[]{:S(2)}) collective-permute-start(bf16[2,4,104,384]{3,2,1,0:T(8,128)(2,1)S(1)} %dynamic-slice_bitcast_fusion.4), channel_id=1, source_target_pairs={{0,16},{4,20},{8,24},{12,28},{16,0},{20,4},{24,8},{28,12},{1,17},{... | collective-permute-start | bytes 1916936 | tf_op jit(solution)/shard_map/ppermute | solution.py:40
  1002.4 21.2 %collective-permute-start.12 = (bf16[1,4,96,384]{3,2,1,0:T(8,128)(2,1)S(1)}, bf16[1,4,96,384]{3,2,1,0:T(8,128)(2,1)S(1)}, u32[]{:S(2)}, u32[]{:S(2)}) collective-permute-start(bf16[1,4,96,384]{3,2,1,0:T(8,128)(2,1)S(1)} %constant_dynamic-slice_fusion.3), channel_id=1, source_target_pairs={{0,16},{4,20},{8,24},{12,28},{16,0},{20,4},{24,8},{28,12},{1,17},{... | collective-permute-start | bytes 884744 | tf_op jit(solution)/shard_map/ppermute | solution.py:40
  1006.1 17.6 %collective-permute-start.14 = (bf16[1,4,104,384]{3,2,1,0:T(8,128)(2,1)}, bf16[1,4,104,384]{3,2,1,0:T(8,128)(2,1)S(1)}, u32[]{:S(2)}, u32[]{:S(2)}) collective-permute-start(bf16[1,4,104,384]{3,2,1,0:T(8,128)(2,1)} %constant_dynamic-slice_fusion.2), channel_id=1, source_target_pairs={{0,8},{4,12},{8,0},{12,4},{16,24},{20,28},{24,16},{28,20},{1,9},{5... | collective-permute-start | bytes 958472 | tf_op jit(solution)/shard_map/ppermute | solution.py:40
  1024.7 57.8 %all-to-all-start.13 = ((bf16[4,200,384]{2,1,0:T(8,128)(2,1)}), bf16[4,200,384]{2,1,0:T(8,128)(2,1)}, u32[]{:S(2)}, u32[]{:S(2)}) async-start(bf16[4,200,384]{2,1,0:T(8,128)(2,1)} %pad_maximum_fusion.11), calls=%async_computation.13 | async-start | bytes 1228800 | tf_op jit(solution)/shard_map/all_to_all | solution.py:134
  1082.5 20.1 %collective-permute-start = (bf16[4,4,200,384]{3,2,1,0:T(8,128)(2,1)}, bf16[4,4,200,384]{3,2,1,0:T(8,128)(2,1)}, u32[]{:S(2)}, u32[]{:S(2)}) collective-permute-start(bf16[4,4,200,384]{3,2,1,0:T(8,128)(2,1)} %dynamic-slice_bitcast_fusion.2), channel_id=1, source_target_pairs={{0,4},{4,0},{8,12},{12,8},{16,20},{20,16},{24,28},{28,24},{1,5},{5... | collective-permute-start | bytes 7372808 | tf_op jit(solution)/shard_map/ppermute | solution.py:40
  1083.7 6.1 collective-permute-start.15
  1085.7 6.9 collective-permute-start.17
  1089.9 9.5 collective-permute-start.16
  1092.6 9.9 collective-permute-start.18
  1106.0 13.8 %collective-permute-start.1 = (bf16[2,4,96,384]{3,2,1,0:T(8,128)(2,1)S(1)}, bf16[2,4,96,384]{3,2,1,0:T(8,128)(2,1)S(1)}, u32[]{:S(2)}, u32[]{:S(2)}) collective-permute-start(bf16[2,4,96,384]{3,2,1,0:T(8,128)(2,1)S(1)} %dynamic-slice_bitcast_fusion.8), channel_id=1, source_target_pairs={{0,8},{4,12},{8,0},{12,4},{16,24},{20,28},{24,16},{28,20},{1,9},{5... | collective-permute-start | bytes 1769480 | tf_op jit(solution)/shard_map/ppermute | solution.py:40
  1106.5 16.0 %collective-permute-start.3 = (bf16[2,4,104,384]{3,2,1,0:T(8,128)(2,1)S(1)}, bf16[2,4,104,384]{3,2,1,0:T(8,128)(2,1)S(1)}, u32[]{:S(2)}, u32[]{:S(2)}) collective-permute-start(bf16[2,4,104,384]{3,2,1,0:T(8,128)(2,1)S(1)} %dynamic-slice_bitcast_fusion.5), channel_id=1, source_target_pairs={{0,16},{4,20},{8,24},{12,28},{16,0},{20,4},{24,8},{28,12},{1,17},{... | collective-permute-start | bytes 1916936 | tf_op jit(solution)/shard_map/ppermute | solution.py:40
  1109.1 33.8 %collective-permute-start.19 = (bf16[4,200,384]{2,1,0:T(8,128)(2,1)}, bf16[4,200,384]{2,1,0:T(8,128)(2,1)}, u32[]{:S(2)}, u32[]{:S(2)}) collective-permute-start(bf16[4,200,384]{2,1,0:T(8,128)(2,1)} %pad_maximum_fusion.12), channel_id=1, source_target_pairs={{0,4},{4,0},{8,12},{12,8},{16,20},{20,16},{24,28},{28,24},{1,5},{5... | collective-permute-start | bytes 1843208 | tf_op jit(solution)/shard_map/ppermute | solution.py:40
  1120.0 7.7 collective-permute-start.2
  1122.7 7.4 collective-permute-start.4
  1131.1 17.8 %all-to-all-start.12 = ((bf16[4,200,384]{2,1,0:T(8,128)(2,1)}), bf16[4,200,384]{2,1,0:T(8,128)(2,1)}, u32[]{:S(2)}, u32[]{:S(2)}) async-start(bf16[4,200,384]{2,1,0:T(8,128)(2,1)} %pad_maximum_fusion.9), calls=%async_computation.12 | async-start | bytes 1228800 | tf_op jit(solution)/shard_map/all_to_all | solution.py:134
  1150.1 5.6 collective-permute-start.5
  1152.5 4.5 collective-permute-start.7
  1155.7 5.2 collective-permute-start.6
  1157.1 5.3 collective-permute-start.8
  1164.1 5.4 collective-permute-start.9
  (166 other events, 714.0 us)
Sparse Core Ops, SparseCore 0:
  29.9 40.4 all-gather.10
  162.8 38.8 all-gather.12
  324.0 38.8 all-gather.14
  645.9 77.3 reduce-scatter.13
  836.8 77.8 reduce-scatter.11
  1023.6 83.0 reduce-scatter.9
